TPU v7x, 32 devices: a whole 2x2x4 slice. The times are simulated.
32 devices in a mesh: dp: 16 (over z, y, core), expert: 2 (over x).
Axes of the slice: x: 2, y: 2, z: 4, core: 2. Of those that a mesh axis runs over, the one named last changes fastest.
Arguments:
- tokens: bfloat16 [4096, 2048], P(('dp', 'expert')), may hold values from -6 to 6
- cotangent: bfloat16 [4096, 2048], P(('dp', 'expert')), may hold values from -6 to 6
- expert_ids: int32 [4096, 8], P(('dp', 'expert')), may hold values from 0 to 127, as said below
- route_weights: float32 [4096, 8], P(('dp', 'expert')), may hold values from 0.1 to 1
- join_groups: int32 [16], replicated, may hold values from 0 to 1
- w_gate: bfloat16 [2048, 1024], P('dp', 'expert'), may hold values from -0.125 to 0.125
- w_up: bfloat16 [2048, 1024], P('dp', 'expert'), may hold values from -0.125 to 0.125
- w_down: bfloat16 [2048, 1024], P('dp', 'expert'), may hold values from -0.1875 to 0.1875
Outputs:
- mixed: bfloat16 [4096, 2048], P(('dp', 'expert'))
- grad_gate: bfloat16 [2048, 1024], P('dp', 'expert')
- grad_up: bfloat16 [2048, 1024], P('dp', 'expert')
- grad_down: bfloat16 [2048, 1024], P('dp', 'expert')
Inputs may be any that keep to these rules, and one draw needn't show every extreme that they name: `expert_ids`: each row names 8 different experts; the rows of one device name expert 0 at most 16 times, and the rows of some device exactly 16 times.
All inputs are finite; a program needn't handle non-finite values.
Results may differ from a plain program's by a relative error of at most 0.014.
Values may be sent and summed in bfloat16 or wider, within the bound.
A program may use at most 64 MiB of HBM per device.

v0:
```python
import functools

import jax
import jax.numpy as jnp
from jax import lax
from jax.experimental import pallas as pl
from jax.experimental.pallas import tpu as pltpu
from jax.sharding import PartitionSpec as P

F32, BF16 = jnp.float32, jnp.bfloat16
MESH = pl.DeviceIdType.MESH
CHUNKS = 2


def dot(a, b, dims):
    return lax.dot_general(a, b, (dims, ((), ())), preferred_element_type=F32)


def kernel(
    pairs, members, cap,
    join, tok, cot, ids, wts, wg, wu, wd,
    mixed, grad_gate, grad_up, grad_down,
    tokv, cotv, wfull, blk, recv1, part, send2, recv_y, mid, recv_z, acc, all3, send4, recv4, gacc, sendg, recvg,
    local, sw, rw, s1, r1, s2y, r2y, s2z, r2z, s3y, r3y, s3z, r3z, s4, r4, sg, rg,
):
    p, j = lax.axis_index("dp"), lax.axis_index("expert")
    pair, core = lax.div(p, 2), lax.rem(p, 2)
    total = pairs * members
    flat = pair * members + j
    partner = (2 * pair + 1 - core, j)
    line, side = lax.div(pair, 2), lax.rem(pair, 2)
    lines = pairs // 2
    across = (2 * (2 * line + 1 - side) + core, j)
    last = lines - 1
    tok_count = tok.shape[0]
    depth, width = wg.shape
    chip_depth = 2 * depth
    rows = members * cap

    def flat_peer(d):
        other = lax.rem(flat + d, total)
        return other, lax.div(other, members), lax.rem(other, members)

    def copy(src, dst, send, recv, device):
        return pltpu.make_async_remote_copy(
            src_ref=src, dst_ref=dst, send_sem=send, recv_sem=recv, device_id=device, device_id_type=MESH
        )

    def on_line(other):
        return (2 * (2 * other + side) + core, j)

    weights = (wg, wu, wd)
    loads = [(cot, cotv), (tok, tokv)] + [(w, wfull.at[n, core]) for n, w in enumerate(weights)]
    loads = [pltpu.make_async_copy(src, dst, local.at[n]) for n, (src, dst) in enumerate(loads)]
    for load in loads:
        load.start()

    barrier = pltpu.get_barrier_semaphore()

    def greet(d, carry):
        _, pair2, j2 = flat_peer(d)
        pl.semaphore_signal(barrier, inc=1, device_id=(2 * pair2 + core, j2), device_id_type=MESH)
        return carry

    lax.fori_loop(1, total, greet, 0)
    pl.semaphore_signal(barrier, inc=1, device_id=partner, device_id_type=MESH)

    chosen = ids[...] == 0
    routed = jnp.max(jnp.where(chosen, 1.0, 0.0), axis=0, keepdims=True)
    weight = jnp.sum(jnp.where(chosen, wts[...], 0.0), axis=0, keepdims=True)
    upper = lax.broadcasted_iota(jnp.int32, (tok_count, tok_count), 0) <= lax.broadcasted_iota(
        jnp.int32, (tok_count, tok_count), 1
    )
    wide = jnp.broadcast_to(routed, (cap, tok_count))
    places = dot(wide.astype(BF16), jnp.where(upper, 1.0, 0.0).astype(BF16), ((1,), (0,))) - 1.0
    slot = lax.broadcasted_iota(jnp.int32, (cap, tok_count), 0).astype(F32)
    pick = jnp.where((places == slot) & (wide > 0.5), 1.0, 0.0)
    slot_weight = jnp.sum(pick * weight, axis=1, keepdims=True)
    spread = pick.T.astype(BF16)
    pick = pick.astype(BF16)
    active = 1.0 - join[p].astype(F32)
    loads[0].wait()
    dpicked_rows = (dot(pick, cotv[...], ((1,), (0,))) * (slot_weight * active)).astype(BF16)
    loads[1].wait()
    picked_rows = dot(pick, tokv[...], ((1,), (0,))).astype(BF16)
    for q in range(pairs):
        cols = slice(q * chip_depth, (q + 1) * chip_depth)
        blk[q, 0] = picked_rows[:, cols]
        blk[q, 1] = dpicked_rows[:, cols]

    pl.semaphore_wait(barrier, total)

    def start1(d, carry):
        _, pair2, j2 = flat_peer(d)
        copy(blk.at[pair2], recv1.at[flat], s1.at[d], r1.at[d], (2 * pair2 + core, j2)).start()
        return carry

    lax.fori_loop(1, total, start1, 0)
    for n, w in enumerate(weights):
        copy(w, wfull.at[n, core], sw.at[n], rw.at[n], partner).start()
    recv1[flat] = blk[pair]
    for n, w in enumerate(weights):
        loads[2 + n].wait()
        copy(w, wfull.at[n, 1 - core], sw.at[n], rw.at[n], partner).wait_recv()

    def wait1(d, carry):
        copy(blk.at[0], recv1.at[lax.rem(flat - d + total, total)], s1.at[d], r1.at[d], partner).wait_recv()
        return carry

    lax.fori_loop(1, total, wait1, 0)

    picked = recv1[:, 0].reshape(total * cap, chip_depth)
    dpicked = recv1[:, 1].reshape(total * cap, chip_depth)
    full = [wfull[n].reshape(chip_depth, width) for n in range(3)]
    for n, left in enumerate((picked, picked, dpicked)):
        term = dot(left, full[n], ((1,), (0,))).reshape(pairs, CHUNKS, rows // CHUNKS, width)
        for h in range(CHUNKS):
            part[h, :, n] = term[:, h]
            send2[h, :, n] = term[:, h].astype(BF16)

    def start2(h, d, carry):
        other, at = lax.rem(line + 1 + d, lines), h * lines + d
        copy(send2.at[h, 2 * other + 1 - side], recv_y.at[h, other], s2y.at[at], r2y.at[at], across).start()
        return carry

    def pass2(h, d, carry):
        other, at = lax.rem(line + 1 + d, lines), h * lines + d
        copy(send2.at[h, 0], recv_y.at[h, other], s2y.at[at], r2y.at[at], across).wait_recv()
        mid[h, other] = (part[h, 2 * other + side] + recv_y[h, other].astype(F32)).astype(BF16)
        copy(mid.at[h, other], recv_z.at[h, line], s2z.at[at], r2z.at[at], on_line(other)).start()
        return carry

    def add2(h, d, carry):
        source, at = lax.rem(line + last - d, lines), h * lines + d
        copy(mid.at[h, 0], recv_z.at[h, source], s2z.at[at], r2z.at[at], across).wait_recv()
        acc[h] += recv_z[h, source].astype(F32)
        return carry

    def start3(h, d, carry):
        other, at = lax.rem(line + 1 + d, lines), h * lines + d
        copy(all3.at[h, pair], all3.at[h, pair], s3z.at[at], r3z.at[at], on_line(other)).start()
        return carry

    def pass3(h, d, carry):
        at = h * lines + d
        held = all3.at[h, 2 * lax.rem(line + last - d, lines) + side]
        copy(all3.at[h, pair], held, s3z.at[at], r3z.at[at], across).wait_recv()
        copy(held, held, s3y.at[at], r3y.at[at], across).start()
        return carry

    def wait3(h, d, carry):
        at = h * lines + d
        place = all3.at[h, 2 * lax.rem(line + last - d, lines) + 1 - side]
        copy(all3.at[h, pair], place, s3y.at[at], r3y.at[at], across).wait_recv()
        return carry

    for h in range(CHUNKS):
        lax.fori_loop(0, lines, functools.partial(start2, h), 0)
    for h in range(CHUNKS):
        lax.fori_loop(0, last, functools.partial(pass2, h), 0)
        at = h * lines + last
        copy(send2.at[h, 0], recv_y.at[h, line], s2y.at[at], r2y.at[at], across).wait_recv()
        acc[h] = part[h, pair] + recv_y[h, line].astype(F32)
    for h in range(CHUNKS):
        lax.fori_loop(0, last, functools.partial(add2, h), 0)
        gate, up, dhidden = acc[h, 0], acc[h, 1], acc[h, 2]
        sig = 1.0 / (1.0 + jnp.exp(-gate))
        all3[h, pair, 0] = (gate * sig * up).astype(BF16)
        all3[h, pair, 1] = (dhidden * up * sig * (1.0 + gate * (1.0 - sig))).astype(BF16)
        all3[h, pair, 2] = (dhidden * gate * sig).astype(BF16)
        lax.fori_loop(0, last, functools.partial(start3, h), 0)
        at = h * lines + last
        copy(all3.at[h, pair], all3.at[h, pair], s3y.at[at], r3y.at[at], across).start()
    for h in range(CHUNKS):
        lax.fori_loop(0, last, functools.partial(pass3, h), 0)
    for h in range(CHUNKS):
        at = h * lines + last
        place = all3.at[h, 2 * line + 1 - side]
        copy(all3.at[h, pair], place, s3y.at[at], r3y.at[at], across).wait_recv()
        lax.fori_loop(0, last, functools.partial(wait3, h), 0)

    hidden, dgate, dup = (
        jnp.stack([all3[h, :, n] for h in range(CHUNKS)], axis=1).reshape(pairs * rows, width) for n in range(3)
    )
    send4[...] = dot(hidden, full[2], ((1,), (1,))).astype(BF16).reshape(total, cap, chip_depth)

    def start4(d, carry):
        other, pair2, j2 = flat_peer(d)
        copy(send4.at[other], recv4.at[j, pair], s4.at[d], r4.at[d], (2 * pair2 + core, j2)).start()
        return carry

    lax.fori_loop(1, total, start4, 0)
    recv4[j, pair] = send4[flat]

    for n, (left, right) in enumerate(((picked, dgate), (picked, dup), (dpicked, hidden))):
        term = dot(left, right, ((0,), (0,))).reshape(2, depth, width)
        gacc[n] = term
        sendg[n] = term.astype(BF16)
        copy(sendg.at[n, 1 - core], recvg.at[n], sg.at[n], rg.at[n], partner).start()

    def wait4(d, carry):
        source = lax.rem(flat - d + total, total)
        place = recv4.at[lax.rem(source, members), lax.div(source, members)]
        copy(send4.at[0], place, s4.at[d], r4.at[d], partner).wait_recv()
        return carry

    lax.fori_loop(1, total, wait4, 0)
    for q in range(pairs):
        out_rows = recv4[0, q].astype(F32)
        for m in range(1, members):
            out_rows += recv4[m, q].astype(F32)
        placed = dot(spread, (out_rows * slot_weight).astype(BF16), ((1,), (0,)))
        mixed[:, q * chip_depth : (q + 1) * chip_depth] = placed.astype(BF16)

    for n, out in enumerate((grad_gate, grad_up, grad_down)):
        copy(sendg.at[n, 0], recvg.at[n], sg.at[n], rg.at[n], partner).wait_recv()
        out[...] = (gacc[n, core] + recvg[n].astype(F32)).astype(BF16)

    for n, w in enumerate(weights):
        copy(w, wfull.at[n, core], sw.at[n], rw.at[n], partner).wait_send()
        copy(sendg.at[n, 0], recvg.at[n], sg.at[n], rg.at[n], partner).wait_send()

    def drain_flat(d, carry):
        copy(blk.at[0], recv1.at[0], s1.at[d], r1.at[d], partner).wait_send()
        copy(send4.at[0], recv4.at[0, 0], s4.at[d], r4.at[d], partner).wait_send()
        return carry

    def drain_y(d, carry):
        copy(send2.at[0, 0], recv_y.at[0, 0], s2y.at[d], r2y.at[d], across).wait_send()
        copy(all3.at[0, 0], all3.at[0, 0], s3y.at[d], r3y.at[d], across).wait_send()
        return carry

    def drain_z(h, d, carry):
        at = h * lines + d
        copy(mid.at[0, 0], recv_z.at[0, 0], s2z.at[at], r2z.at[at], across).wait_send()
        copy(all3.at[0, 0], all3.at[0, 0], s3z.at[at], r3z.at[at], across).wait_send()
        return carry

    lax.fori_loop(1, total, drain_flat, 0)
    lax.fori_loop(0, CHUNKS * lines, drain_y, 0)
    for h in range(CHUNKS):
        lax.fori_loop(0, last, functools.partial(drain_z, h), 0)


def per_device(pairs, members, tokens, cotangent, expert_ids, route_weights, join_groups, w_gate, w_up, w_down):
    tok_count, model = tokens.shape
    depth, width = w_gate.shape
    cap = tok_count // 8
    total = pairs * members
    rows = members * cap
    vmem = pl.BlockSpec(memory_space=pltpu.VMEM)
    hbm = pl.BlockSpec(memory_space=pl.ANY)
    lines = pairs // 2
    dma = pltpu.SemaphoreType.DMA
    grad = jax.ShapeDtypeStruct((depth, width), BF16)
    return pl.pallas_call(
        functools.partial(kernel, pairs, members, cap),
        out_shape=(jax.ShapeDtypeStruct((tok_count, model), BF16), grad, grad, grad),
        in_specs=[pl.BlockSpec(memory_space=pltpu.SMEM), hbm, hbm, vmem, vmem, hbm, hbm, hbm],
        out_specs=(vmem,) * 4,
        scratch_shapes=[
            pltpu.VMEM((tok_count, model), BF16),
            pltpu.VMEM((tok_count, model), BF16),
            pltpu.VMEM((3, 2, depth, width), BF16),
            pltpu.VMEM((pairs, 2, cap, 2 * depth), BF16),
            pltpu.VMEM((total, 2, cap, 2 * depth), BF16),
            pltpu.VMEM((CHUNKS, pairs, 3, rows // CHUNKS, width), F32),
            pltpu.VMEM((CHUNKS, pairs, 3, rows // CHUNKS, width), BF16),
            pltpu.VMEM((CHUNKS, lines, 3, rows // CHUNKS, width), BF16),
            pltpu.VMEM((CHUNKS, lines, 3, rows // CHUNKS, width), BF16),
            pltpu.VMEM((CHUNKS, lines, 3, rows // CHUNKS, width), BF16),
            pltpu.VMEM((CHUNKS, 3, rows // CHUNKS, width), F32),
            pltpu.VMEM((CHUNKS, pairs, 3, rows // CHUNKS, width), BF16),
            pltpu.VMEM((total, cap, 2 * depth), BF16),
            pltpu.VMEM((members, pairs, cap, 2 * depth), BF16),
            pltpu.VMEM((3, 2, depth, width), F32),
            pltpu.VMEM((3, 2, depth, width), BF16),
            pltpu.VMEM((3, depth, width), BF16),
            dma((5,)),
            dma((3,)), dma((3,)),
            dma((total,)), dma((total,)),
            dma((CHUNKS * lines,)), dma((CHUNKS * lines,)),
            dma((CHUNKS * lines,)), dma((CHUNKS * lines,)),
            dma((CHUNKS * lines,)), dma((CHUNKS * lines,)),
            dma((CHUNKS * lines,)), dma((CHUNKS * lines,)),
            dma((total,)), dma((total,)),
            dma((3,)), dma((3,)),
        ],
        compiler_params=pltpu.CompilerParams(
            collective_id=0, has_side_effects=True, vmem_limit_bytes=60 * 1024 * 1024
        ),
        name="expert_step",
    )(join_groups, tokens, cotangent, expert_ids.T, route_weights.T, w_gate, w_up, w_down)


def solution(mesh):
    in_specs = (
        P(("dp", "expert"), None),
        P(("dp", "expert"), None),
        P(("dp", "expert"), None),
        P(("dp", "expert"), None),
        P(),
        P("dp", "expert"),
        P("dp", "expert"),
        P("dp", "expert"),
    )
    out_specs = (P(("dp", "expert"), None), P("dp", "expert"), P("dp", "expert"), P("dp", "expert"))
    body = functools.partial(per_device, mesh.shape["dp"] // 2, mesh.shape["expert"])
    return jax.shard_map(body, mesh=mesh, in_specs=in_specs, out_specs=out_specs, check_vma=False)
```

profile of v0, /device:TPU:0, one launch (start us, length us, event | category | flops | bytes accessed | tf_op | source)
XLA Modules:
  0.0 55.0 jit_solution(11978755348898964627)
XLA Ops:
  0.6 49.9 %expert_step.1 = (bf16[128,2048]{1,0:T(8,128)(2,1)}, bf16[128,512]{1,0:T(8,128)(2,1)}, bf16[128,512]{1,0:T(8,128)(2,1)}, bf16[128,512]{1,0:T(8,128)(2,1)}) custom-call(s32[16]{0:T(128)} %join.1, bf16[128,2048]{1,0:T(8,128)(2,1)} %tok.1, bf16[128,2048]{1,0:T(8,128)(2,1)} %cot.1, s32[8,128]{1,0:T(8,128)} %bitcast.2, f32[8,128]{1,0:T(8,128)} %bitcast.3, ...), custom_call_target="tpu_custom_call" | custom-call | tf_op jit(solution)/shard_map/expert_step/pallas_call | solution.py:256
  50.5 0.0 copy-start.2
  50.5 1.9 %copy.16 = bf16[128,2048]{1,0:T(8,128)(2,1)} copy(bf16[128,2048]{1,0:T(8,128)(2,1)} %get-tuple-element.8) | data formatting | bytes 1048576
  52.5 0.0 copy-done.2
  52.5 0.0 copy-start.1
  52.5 0.7 %copy.17 = bf16[128,512]{1,0:T(8,128)(2,1)} copy(bf16[128,512]{1,0:T(8,128)(2,1)S(1)} %copy-done.2) | data formatting | bytes 262144
  53.1 0.3 copy-done.1
  53.4 0.0 copy-start
  53.4 0.7 %copy.18 = bf16[128,512]{1,0:T(8,128)(2,1)} copy(bf16[128,512]{1,0:T(8,128)(2,1)S(1)} %copy-done.1) | data formatting | bytes 262144
  54.1 0.3 copy-done
  54.4 0.7 %copy.19 = bf16[128,512]{1,0:T(8,128)(2,1)} copy(bf16[128,512]{1,0:T(8,128)(2,1)S(1)} %copy-done) | data formatting | bytes 262144
Async XLA Ops:
  50.5 1.9 %copy-start.2 = (bf16[128,512]{1,0:T(8,128)(2,1)S(1)}, bf16[128,512]{1,0:T(8,128)(2,1)}, u32[]{:S(2)}) copy-start(bf16[128,512]{1,0:T(8,128)(2,1)} %get-tuple-element.9) | copy-start | bytes 393220
  52.5 1.0 %copy-start.1 = (bf16[128,512]{1,0:T(8,128)(2,1)S(1)}, bf16[128,512]{1,0:T(8,128)(2,1)}, u32[]{:S(2)}) copy-start(bf16[128,512]{1,0:T(8,128)(2,1)} %get-tuple-element.10) | copy-start | bytes 393220
  53.4 1.0 %copy-start = (bf16[128,512]{1,0:T(8,128)(2,1)S(1)}, bf16[128,512]{1,0:T(8,128)(2,1)}, u32[]{:S(2)}) copy-start(bf16[128,512]{1,0:T(8,128)(2,1)} %get-tuple-element.11) | copy-start | bytes 393220
where the time goes:
time: 55.2 us; the launch traced here: 55 us
  Pallas kernels  49.9 us (90%)
  local copies, waits for them, and re-layouts  4.48 us (8%)
  between operations  0.65 us (1%)
    pallas_call x1, Pallas kernels, per_device(): pl.pallas_call(functools.partial(kernel, pairs, members, cap), out_shape=...  49.9 us
    unnamed x10, local copies, waits for them, and re-layouts  4.48 us

commit v1 on v0

--- a/solution.py
+++ b/solution.py
@@ -242,6 +242,15 @@
         lax.fori_loop(0, last, functools.partial(drain_z, h), 0)
 
 
+def write_out(*refs):
+    sems = refs[-1]
+    copies = [pltpu.make_async_copy(refs[n], refs[4 + n], sems.at[n]) for n in range(4)]
+    for c in copies:
+        c.start()
+    for c in copies:
+        c.wait()
+
+
 def per_device(pairs, members, tokens, cotangent, expert_ids, route_weights, join_groups, w_gate, w_up, w_down):
     tok_count, model = tokens.shape
     depth, width = w_gate.shape
@@ -252,10 +261,10 @@
     hbm = pl.BlockSpec(memory_space=pl.ANY)
     lines = pairs // 2
     dma = pltpu.SemaphoreType.DMA
-    grad = jax.ShapeDtypeStruct((depth, width), BF16)
-    return pl.pallas_call(
+    grad = pltpu.VMEM((depth, width), BF16)
+    held = pl.pallas_call(
         functools.partial(kernel, pairs, members, cap),
-        out_shape=(jax.ShapeDtypeStruct((tok_count, model), BF16), grad, grad, grad),
+        out_shape=(pltpu.VMEM((tok_count, model), BF16), grad, grad, grad),
         in_specs=[pl.BlockSpec(memory_space=pltpu.SMEM), hbm, hbm, vmem, vmem, hbm, hbm, hbm],
         out_specs=(vmem,) * 4,
         scratch_shapes=[
@@ -291,6 +300,14 @@
         ),
         name="expert_step",
     )(join_groups, tokens, cotangent, expert_ids.T, route_weights.T, w_gate, w_up, w_down)
+    return pl.pallas_call(
+        write_out,
+        out_shape=tuple(jax.ShapeDtypeStruct(h.shape, h.dtype) for h in held),
+        in_specs=[vmem] * 4,
+        out_specs=(hbm,) * 4,
+        scratch_shapes=[dma((4,))],
+        name="write_out",
+    )(*(pltpu.with_memory_space_constraint(h, pltpu.VMEM) for h in held))
 
 
 def solution(mesh):

time: 55.2 us -> 50.7 us (0.918)
  local copies, waits for them, and re-layouts: 4.48 us -> 0 us
    unnamed x10 -> x0, local copies, waits for them, and re-layouts: 4.48 us -> none
    pallas_call x0 -> x1, Pallas kernels: none -> 0.95 us  [per_device(): pl.pallas_call(write_out, out_shape=tuple((jax.ShapeDtypeStruct(h.shape,...]
    pallas_call x1, Pallas kernels: 49.9 us -> 48.9 us  [per_device(): pl.pallas_call(functools.partial(kernel, pairs, members, cap), out_shape=...]
where the time goes in v1:
time: 50.7 us; the launch traced here: 50.5 us
  Pallas kernels  49.9 us (98%)
  between operations  0.64 us (1%)
    pallas_call x1, Pallas kernels, per_device(): pl.pallas_call(functools.partial(kernel, pairs, members, cap), out_shape=...  48.9 us

profile of v1, /device:TPU:0, one launch (start us, length us, event | category | flops | bytes accessed | tf_op | source)
XLA Modules:
  0.0 50.5 jit_solution(9604536418524387445)
XLA Ops:
  0.6 48.9 %expert_step.1 = (bf16[128,2048]{1,0:T(8,128)(2,1)S(1)}, bf16[128,512]{1,0:T(8,128)(2,1)S(1)}, bf16[128,512]{1,0:T(8,128)(2,1)S(1)}, bf16[128,512]{1,0:T(8,128)(2,1)S(1)}) custom-call(s32[16]{0:T(128)} %join.1, bf16[128,2048]{1,0:T(8,128)(2,1)} %tok.1, bf16[128,2048]{1,0:T(8,128)(2,1)} %cot.1, s32[8,128]{1,0:T(8,128)} %bitcast.2, f32[8,128]{1,0:T(8,128)} %bitcast.3, ...), custom_call_target="tpu_custom_call" | custom-call | tf_op jit(solution)/shard_map/expert_step/pallas_call | solution.py:265
  49.6 1.0 %write_out.1 = (bf16[128,2048]{1,0:T(8,128)(2,1)}, bf16[128,512]{1,0:T(8,128)(2,1)}, bf16[128,512]{1,0:T(8,128)(2,1)}, bf16[128,512]{1,0:T(8,128)(2,1)}) custom-call(bf16[128,2048]{1,0:T(8,128)(2,1)S(1)} %get-tuple-element.8.refs_0_, bf16[128,512]{1,0:T(8,128)(2,1)S(1)} %get-tuple-element.9.refs_1_, bf16[128,512]{1,0:T(8,128)(2,1)S(1)} %get-tuple-element.10.refs_2_, ...), custom_call_target="tpu_custom_call" | custom-call | tf_op jit(solution)/shard_map/write_out/pallas_call | solution.py:303

commit v2 on v1

v2 whole, which is shorter than its diff:
```python
import functools

import jax
import jax.numpy as jnp
from jax import lax
from jax.experimental import pallas as pl
from jax.experimental.pallas import tpu as pltpu
from jax.sharding import PartitionSpec as P

F32, BF16 = jnp.float32, jnp.bfloat16
MESH = pl.DeviceIdType.MESH


def dot(a, b, dims):
    return lax.dot_general(a, b, (dims, ((), ())), preferred_element_type=F32)


def flip(a, d, count):
    out, bit = 0, 1
    while bit < count:
        mine = lax.rem(lax.div(a, bit), 2)
        turn = (d // bit) % 2 if isinstance(d, int) else lax.rem(lax.div(d, bit), 2)
        out += bit * (mine + turn - 2 * mine * turn)
        bit *= 2
    return out


def each(low, high, body):
    if high - low <= 16:
        for i in range(low, high):
            body(i)
    else:
        lax.fori_loop(low, high, lambda i, carry: (body(i), carry)[1], 0)


def kernel(
    lines, members, cap,
    join, tok, cot, ids, wts, wg, wu, wd,
    mixed, grad_gate, grad_up, grad_down,
    tokv, cotv, wfull, blk, recv1, rows_all, part, send2, recv2, all3, send4, recv4,
    local, swy, rwy, swc, rwc, swf, rwf, s1, r1, sx, rx, s2, r2, s3z, r3z, s3y, r3y, s3c, r3c, s4, r4,
):
    p, j = lax.axis_index("dp"), lax.axis_index("expert")
    line, side, core = lax.div(p, 4), lax.rem(lax.div(p, 2), 2), lax.rem(p, 2)
    quarter = 2 * side + core
    total = lines * members
    flat = line * members + j
    tok_count = tok.shape[0]
    depth, width = wg.shape
    line_depth = 4 * depth

    def device(z, y, c, member):
        return (4 * z + 2 * y + c, member)

    partner = device(line, side, 1 - core, j)
    across = device(line, 1 - side, core, j)

    def copy(src, dst, send, recv, target):
        return pltpu.make_async_remote_copy(
            src_ref=src, dst_ref=dst, send_sem=send, recv_sem=recv, device_id=target, device_id_type=MESH
        )

    def peer(t):
        if isinstance(t, int):
            dz, dj = t // members, t % members
        else:
            dz, dj = lax.div(t, members), lax.rem(t, members)
        return flip(line, dz, lines), flip(j, dj, members)

    def on_line(d):
        z = flip(line, d, lines)
        return z, device(z, side, core, j)

    near = [(0, 1), (1, 0), (1, 1)]

    def beside(n):
        y = 1 - side if near[n][0] else side
        c = 1 - core if near[n][1] else core
        return 2 * y + c, device(line, y, c, j)

    weights = (wg, wu, wd)
    loads = [(cot, cotv), (tok, tokv)] + [(w, wfull.at[n, quarter]) for n, w in enumerate(weights)]
    loads = [pltpu.make_async_copy(src, dst, local.at[n]) for n, (src, dst) in enumerate(loads)]
    for load in loads:
        load.start()

    barrier = pltpu.get_barrier_semaphore()

    def greet(t):
        z, member = peer(t)
        pl.semaphore_signal(barrier, inc=1, device_id=device(z, side, core, member), device_id_type=MESH)

    each(1, total, greet)
    for n in range(3):
        pl.semaphore_signal(barrier, inc=1, device_id=beside(n)[1], device_id_type=MESH)

    chosen = ids[...] == 0
    routed = jnp.max(jnp.where(chosen, 1.0, 0.0), axis=0, keepdims=True)
    weight = jnp.sum(jnp.where(chosen, wts[...], 0.0), axis=0, keepdims=True)
    upper = lax.broadcasted_iota(jnp.int32, (tok_count, tok_count), 0) <= lax.broadcasted_iota(
        jnp.int32, (tok_count, tok_count), 1
    )
    wide = jnp.broadcast_to(routed, (cap, tok_count))
    places = dot(wide.astype(BF16), jnp.where(upper, 1.0, 0.0).astype(BF16), ((1,), (0,))) - 1.0
    slot = lax.broadcasted_iota(jnp.int32, (cap, tok_count), 0).astype(F32)
    pick = jnp.where((places == slot) & (wide > 0.5), 1.0, 0.0)
    slot_weight = jnp.sum(pick * weight, axis=1, keepdims=True)
    spread = pick.T.astype(BF16)
    pick = pick.astype(BF16)
    active = 1.0 - join[p].astype(F32)
    loads[0].wait()
    dpicked_rows = (dot(pick, cotv[...], ((1,), (0,))) * (slot_weight * active)).astype(BF16)
    loads[1].wait()
    picked_rows = dot(pick, tokv[...], ((1,), (0,))).astype(BF16)
    for n, taken in enumerate((picked_rows, dpicked_rows)):
        for z in range(lines):
            for k in range(4):
                at = z * line_depth + k * depth
                blk[n, z, k] = taken[:, at : at + depth]
    for n in range(3):
        loads[2 + n].wait()

    pl.semaphore_wait(barrier, total - 1 + 3)

    def swap(n):
        return copy(wfull.at[n, quarter], wfull.at[n, quarter], swy.at[n], rwy.at[n], across)

    def lend(n):
        return copy(wfull.at[n, quarter], wfull.at[n, quarter], swc.at[n], rwc.at[n], partner)

    def relay(n):
        held = wfull.at[n, 2 * (1 - side) + core]
        return copy(held, held, swf.at[n], rwf.at[n], partner)

    def give(q, t):
        z, member = peer(t)
        return copy(blk.at[q, z], recv1.at[q, flat], s1.at[q, t], r1.at[q, t], device(z, side, core, member))

    def take(q, t):
        z, member = peer(t)
        place = recv1.at[q, z * members + member]
        copy(blk.at[q, 0], place, s1.at[q, t], r1.at[q, t], partner).wait_recv()

    def weights_in(n):
        swap(n).wait_recv()
        relay(n).start()
        lend(n).wait_recv()

    swap(0).start()
    each(1, total, lambda t: give(0, t).start())
    lend(0).start()
    swap(1).start()
    swap(2).start()
    each(1, total, lambda t: give(1, t).start())
    lend(1).start()
    lend(2).start()
    for q in range(2):
        recv1[q, flat] = blk[q, line]

    def product(n, q):
        left = jnp.concatenate([recv1[q, :, k].reshape(total * cap, depth) for k in range(4)], axis=1)
        term = dot(left, wfull[n].reshape(line_depth, width), ((1,), (0,)))
        term = term.reshape(lines, members * cap, width)
        part[n] = term
        send2[n] = term.astype(BF16)
        for d in range(1, lines):
            z, there = on_line(d)
            copy(send2.at[n, z], recv2.at[n, line], s2.at[n, d], r2.at[n, d], there).start()

    def summed(n):
        total_rows = part[n, line]
        for d in range(1, lines):
            z, there = on_line(d)
            copy(send2.at[n, 0], recv2.at[n, z], s2.at[n, d], r2.at[n, d], there).wait_recv()
            total_rows += recv2[n, z].astype(F32)
        return total_rows

    weights_in(0)
    each(1, total, functools.partial(take, 0))
    relay(0).wait_recv()
    product(0, 0)
    weights_in(1)
    relay(1).wait_recv()
    product(1, 0)
    weights_in(2)
    each(1, total, functools.partial(take, 1))
    relay(2).wait_recv()
    product(2, 1)

    def share(q, n):
        k, there = beside(n)
        return copy(recv1.at[q, :, k], rows_all.at[q, quarter], sx.at[q, n], rx.at[q, n], there)

    for q in range(2):
        for n in range(3):
            share(q, n).start()
        rows_all[q, quarter] = recv1[q, :, quarter]

    def held(n, z):
        return all3.at[n, quarter, z]

    def spread_out(n):
        for d in range(1, lines):
            _, there = on_line(d)
            copy(held(n, line), held(n, line), s3z.at[n, d], r3z.at[n, d], there).start()
        copy(held(n, line), held(n, line), s3y.at[n, 0], r3y.at[n, 0], across).start()

    def pass_on(n):
        for d in range(1, lines):
            z, there = on_line(d)
            copy(held(n, line), held(n, z), s3z.at[n, d], r3z.at[n, d], there).wait_recv()
            copy(held(n, z), held(n, z), s3y.at[n, d], r3y.at[n, d], across).start()
        mine = all3.at[n, quarter]
        copy(mine, mine, s3c.at[n, 0], r3c.at[n, 0], partner).start()

    def from_across(n):
        other = 2 * (1 - side) + core
        for d in range(lines):
            z, _ = on_line(d)
            copy(held(n, line), all3.at[n, other, z], s3y.at[n, d], r3y.at[n, d], across).wait_recv()
        theirs = all3.at[n, other]
        copy(theirs, theirs, s3c.at[n, 1], r3c.at[n, 1], partner).start()

    def from_partner(n):
        for h, y in enumerate((side, 1 - side)):
            place = all3.at[n, 2 * y + 1 - core]
            copy(place, place, s3c.at[n, h], r3c.at[n, h], partner).wait_recv()

    gate, up = summed(0), summed(1)
    sig = 1.0 / (1.0 + jnp.exp(-gate))
    all3[0, quarter, line] = (gate * sig * up).astype(BF16)
    spread_out(0)
    dhidden = summed(2)
    all3[1, quarter, line] = (dhidden * up * sig * (1.0 + gate * (1.0 - sig))).astype(BF16)
    spread_out(1)
    all3[2, quarter, line] = (dhidden * gate * sig).astype(BF16)
    spread_out(2)

    pass_on(0)
    hidden = all3[0, quarter].reshape(total * cap, width)
    out = dot(hidden, wfull[2].reshape(line_depth, width), ((1,), (1,)))
    send4[...] = out.astype(BF16).reshape(total, cap, line_depth)

    def return_rows(t):
        z, member = peer(t)
        there = device(z, side, core, member)
        return copy(send4.at[z * members + member], recv4.at[j, line], s4.at[t], r4.at[t], there)

    each(1, total, lambda t: return_rows(t).start())
    recv4[j, line] = send4[flat]
    pass_on(1)
    pass_on(2)
    for q in range(2):
        for n in range(3):
            k, there = beside(n)
            copy(rows_all.at[q, 0], rows_all.at[q, k], sx.at[q, n], rx.at[q, n], there).wait_recv()

    def gradient(n, q, result):
        from_partner(n)
        left = rows_all[q].reshape(4 * total * cap, depth)
        result[...] = dot(left, all3[n].reshape(4 * total * cap, width), ((0,), (0,))).astype(BF16)

    from_across(0)
    gradient(0, 1, grad_down)
    from_across(1)
    gradient(1, 0, grad_gate)
    from_across(2)

    def rows_back(t):
        z, member = peer(t)
        copy(send4.at[0], recv4.at[member, z], s4.at[t], r4.at[t], partner).wait_recv()

    each(1, total, rows_back)
    for z in range(lines):
        out_rows = recv4[0, z].astype(F32)
        for m in range(1, members):
            out_rows += recv4[m, z].astype(F32)
        placed = dot(spread, (out_rows * slot_weight).astype(BF16), ((1,), (0,)))
        mixed[:, z * line_depth : (z + 1) * line_depth] = placed.astype(BF16)
    gradient(2, 0, grad_up)

    def sent(t):
        for q in range(2):
            copy(blk.at[q, 0], recv1.at[q, 0], s1.at[q, t], r1.at[q, t], partner).wait_send()
        copy(send4.at[0], recv4.at[0, 0], s4.at[t], r4.at[t], partner).wait_send()

    each(1, total, sent)
    for n in range(3):
        swap(n).wait_send()
        lend(n).wait_send()
        relay(n).wait_send()
        for q in range(2):
            share(q, n).wait_send()
        for d in range(1, lines):
            copy(send2.at[n, 0], recv2.at[n, 0], s2.at[n, d], r2.at[n, d], partner).wait_send()
            copy(held(n, 0), held(n, 0), s3z.at[n, d], r3z.at[n, d], partner).wait_send()
        for d in range(lines):
            copy(held(n, 0), held(n, 0), s3y.at[n, d], r3y.at[n, d], across).wait_send()
        for h in range(2):
            copy(all3.at[n, 0], all3.at[n, 0], s3c.at[n, h], r3c.at[n, h], partner).wait_send()


def write_out(*refs):
    sems = refs[-1]
    copies = [pltpu.make_async_copy(refs[n], refs[4 + n], sems.at[n]) for n in range(4)]
    for c in copies:
        c.start()
    for c in copies:
        c.wait()


def per_device(lines, members, tokens, cotangent, expert_ids, route_weights, join_groups, w_gate, w_up, w_down):
    tok_count, model = tokens.shape
    depth, width = w_gate.shape
    cap = tok_count // 8
    total = lines * members
    rows = members * cap
    vmem = pl.BlockSpec(memory_space=pltpu.VMEM)
    hbm = pl.BlockSpec(memory_space=pl.ANY)
    dma = pltpu.SemaphoreType.DMA
    grad = pltpu.VMEM((depth, width), BF16)
    results = pl.pallas_call(
        functools.partial(kernel, lines, members, cap),
        out_shape=(pltpu.VMEM((tok_count, model), BF16), grad, grad, grad),
        in_specs=[pl.BlockSpec(memory_space=pltpu.SMEM), hbm, hbm, vmem, vmem, hbm, hbm, hbm],
        out_specs=(vmem,) * 4,
        scratch_shapes=[
            pltpu.VMEM((tok_count, model), BF16),
            pltpu.VMEM((tok_count, model), BF16),
            pltpu.VMEM((3, 4, depth, width), BF16),
            pltpu.VMEM((2, lines, 4, cap, depth), BF16),
            pltpu.VMEM((2, total, 4, cap, depth), BF16),
            pltpu.VMEM((2, 4, total, cap, depth), BF16),
            pltpu.VMEM((3, lines, rows, width), F32),
            pltpu.VMEM((3, lines, rows, width), BF16),
            pltpu.VMEM((3, lines, rows, width), BF16),
            pltpu.VMEM((3, 4, lines, rows, width), BF16),
            pltpu.VMEM((total, cap, 4 * depth), BF16),
            pltpu.VMEM((members, lines, cap, 4 * depth), BF16),
            dma((5,)),
            dma((3,)), dma((3,)), dma((3,)), dma((3,)), dma((3,)), dma((3,)),
            dma((2, total)), dma((2, total)),
            dma((2, 3)), dma((2, 3)),
            dma((3, lines)), dma((3, lines)),
            dma((3, lines)), dma((3, lines)),
            dma((3, lines)), dma((3, lines)),
            dma((3, 2)), dma((3, 2)),
            dma((total,)), dma((total,)),
        ],
        compiler_params=pltpu.CompilerParams(
            collective_id=0, has_side_effects=True, vmem_limit_bytes=60 * 1024 * 1024
        ),
        name="expert_step",
    )(join_groups, tokens, cotangent, expert_ids.T, route_weights.T, w_gate, w_up, w_down)
    return pl.pallas_call(
        write_out,
        out_shape=tuple(jax.ShapeDtypeStruct(r.shape, r.dtype) for r in results),
        in_specs=[vmem] * 4,
        out_specs=(hbm,) * 4,
        scratch_shapes=[dma((4,))],
        name="write_out",
    )(*(pltpu.with_memory_space_constraint(r, pltpu.VMEM) for r in results))


def solution(mesh):
    in_specs = (
        P(("dp", "expert"), None),
        P(("dp", "expert"), None),
        P(("dp", "expert"), None),
        P(("dp", "expert"), None),
        P(),
        P("dp", "expert"),
        P("dp", "expert"),
        P("dp", "expert"),
    )
    out_specs = (P(("dp", "expert"), None), P("dp", "expert"), P("dp", "expert"), P("dp", "expert"))
    body = functools.partial(per_device, mesh.shape["dp"] // 4, mesh.shape["expert"])
    return jax.shard_map(body, mesh=mesh, in_specs=in_specs, out_specs=out_specs, check_vma=False)
```

time: 50.7 us -> 40.6 us (0.80)
  Pallas kernels: 49.9 us -> 39.5 us
    pallas_call x2, Pallas kernels: 49.9 us -> 39.5 us  [the longest x1 38.6 us: per_device(): pl.pallas_call(functools.partial(kernel, lines, members, cap), out_shape=...]
where the time goes in v2:
time: 40.6 us; the launch traced here: 40.2 us
  Pallas kernels  39.5 us (97%)
  between operations  0.64 us (2%)
    pallas_call x1, Pallas kernels, per_device(): pl.pallas_call(functools.partial(kernel, lines, members, cap), out_shape=...  38.6 us
    pallas_call x1, Pallas kernels, per_device(): pl.pallas_call(write_out, out_shape=tuple((jax.ShapeDtypeStruct(r.shape,...  0.95 us

profile of v2, /device:TPU:0, one launch (start us, length us, event | category | flops | bytes accessed | tf_op | source)
XLA Modules:
  0.0 40.2 jit_solution(2866507836831046196)
XLA Ops:
  0.6 38.6 %expert_step.1 = (bf16[128,2048]{1,0:T(8,128)(2,1)S(1)}, bf16[128,512]{1,0:T(8,128)(2,1)S(1)}, bf16[128,512]{1,0:T(8,128)(2,1)S(1)}, bf16[128,512]{1,0:T(8,128)(2,1)S(1)}) custom-call(s32[16]{0:T(128)} %join.1, bf16[128,2048]{1,0:T(8,128)(2,1)} %tok.1, bf16[128,2048]{1,0:T(8,128)(2,1)} %cot.1, s32[8,128]{1,0:T(8,128)} %bitcast.2, f32[8,128]{1,0:T(8,128)} %bitcast.3, ...), custom_call_target="tpu_custom_call" | custom-call | tf_op jit(solution)/shard_map/expert_step/pallas_call | solution.py:322
  39.2 1.0 %write_out.1 = (bf16[128,2048]{1,0:T(8,128)(2,1)}, bf16[128,512]{1,0:T(8,128)(2,1)}, bf16[128,512]{1,0:T(8,128)(2,1)}, bf16[128,512]{1,0:T(8,128)(2,1)}) custom-call(bf16[128,2048]{1,0:T(8,128)(2,1)S(1)} %get-tuple-element.8.refs_0_, bf16[128,512]{1,0:T(8,128)(2,1)S(1)} %get-tuple-element.9.refs_1_, bf16[128,512]{1,0:T(8,128)(2,1)S(1)} %get-tuple-element.10.refs_2_, ...), custom_call_target="tpu_custom_call" | custom-call | tf_op jit(solution)/shard_map/write_out/pallas_call | solution.py:355

commit v3 on v2

v3 whole, which is shorter than its diff:
```python
import functools

import jax
import jax.numpy as jnp
from jax import lax
from jax.experimental import pallas as pl
from jax.experimental.pallas import tpu as pltpu
from jax.sharding import PartitionSpec as P

F32, BF16 = jnp.float32, jnp.bfloat16
MESH = pl.DeviceIdType.MESH


def dot(a, b, dims):
    return lax.dot_general(a, b, (dims, ((), ())), preferred_element_type=F32)


def flip(a, d, count):
    out, bit = 0, 1
    while bit < count:
        mine = lax.rem(lax.div(a, bit), 2)
        turn = (d // bit) % 2 if isinstance(d, int) else lax.rem(lax.div(d, bit), 2)
        out += bit * (mine + turn - 2 * mine * turn)
        bit *= 2
    return out


def each(low, high, body):
    if high - low <= 16:
        for i in range(low, high):
            body(i)
    else:
        lax.fori_loop(low, high, lambda i, carry: (body(i), carry)[1], 0)


def kernel(
    lines, members, cap,
    join, tok, cot, ids, wts, wg, wu, wd,
    mixed, grad_gate, grad_up, grad_down,
    joinv, idv, wtv, tokv, cotv, wfull, blk, recv1, rows_all, part, send2, recv2, all3, send4, recv4,
    local, out, rwy, rwp, r1, rx, r2, r3z, r3y, r3c, r4,
):
    p, j = lax.axis_index("dp"), lax.axis_index("expert")
    line, side, core = lax.div(p, 4), lax.rem(lax.div(p, 2), 2), lax.rem(p, 2)
    quarter = 2 * side + core
    total = lines * members
    flat = line * members + j
    tok_count = tok.shape[0]
    depth, width = wg.shape
    line_depth = 4 * depth

    def device(z, y, c, member):
        return (4 * z + 2 * y + c, member)

    partner = device(line, side, 1 - core, j)
    across = device(line, 1 - side, core, j)

    def copy(src, dst, send, recv, target):
        return pltpu.make_async_remote_copy(
            src_ref=src, dst_ref=dst, send_sem=send, recv_sem=recv, device_id=target, device_id_type=MESH
        )

    def peer(t):
        if isinstance(t, int):
            dz, dj = t // members, t % members
        else:
            dz, dj = lax.div(t, members), lax.rem(t, members)
        return flip(line, dz, lines), flip(j, dj, members)

    def on_line(d):
        z = flip(line, d, lines)
        return z, device(z, side, core, j)

    near = [(0, 1), (1, 0), (1, 1)]

    def beside(n):
        y = 1 - side if near[n][0] else side
        c = 1 - core if near[n][1] else core
        return 2 * y + c, device(line, y, c, j)

    barrier = pltpu.get_barrier_semaphore()

    def greet(t):
        z, member = peer(t)
        pl.semaphore_signal(barrier, inc=1, device_id=device(z, side, core, member), device_id_type=MESH)

    each(1, total, greet)
    for n in range(3):
        pl.semaphore_signal(barrier, inc=1, device_id=beside(n)[1], device_id_type=MESH)

    loads = [
        pltpu.make_async_copy(src, dst, local.at[n])
        for n, (src, dst) in enumerate(((ids, idv), (wts, wtv), (join, joinv), (tok, tokv), (cot, cotv)))
    ]
    own = [pltpu.make_async_copy(w, wfull.at[n, quarter], local.at[5]) for n, w in enumerate((wg, wu, wd))]
    for load in loads[:3] + own + loads[3:]:
        load.start()
    for load in loads[:2]:
        load.wait()

    chosen = idv[...] == 0
    routed = jnp.max(jnp.where(chosen, 1.0, 0.0), axis=0, keepdims=True)
    weight = jnp.sum(jnp.where(chosen, wtv[...], 0.0), axis=0, keepdims=True)
    upper = lax.broadcasted_iota(jnp.int32, (tok_count, tok_count), 0) <= lax.broadcasted_iota(
        jnp.int32, (tok_count, tok_count), 1
    )
    wide = jnp.broadcast_to(routed, (cap, tok_count))
    places = dot(wide.astype(BF16), jnp.where(upper, 1.0, 0.0).astype(BF16), ((1,), (0,))) - 1.0
    slot = lax.broadcasted_iota(jnp.int32, (cap, tok_count), 0).astype(F32)
    pick = jnp.where((places == slot) & (wide > 0.5), 1.0, 0.0)
    slot_weight = jnp.sum(pick * weight, axis=1, keepdims=True)
    spread = pick.T.astype(BF16)
    pick = pick.astype(BF16)
    loads[2].wait()
    active = 1.0 - joinv[p].astype(F32)
    mine = wfull.at[:, quarter]
    pltpu.make_async_copy(mine, mine, local.at[5]).wait()

    def swap(n):
        return copy(wfull.at[n, quarter], wfull.at[n, quarter], out.at[0], rwy.at[n], across)

    def lend(n):
        return copy(wfull.at[n, quarter], wfull.at[n, quarter], out.at[1], rwp.at[n], partner)

    def relay(n):
        held = wfull.at[n, 2 * (1 - side) + core]
        return copy(held, held, out.at[2], rwp.at[n], partner)

    def give(q, t):
        z, member = peer(t)
        copy(blk.at[q, z], recv1.at[q, flat], out.at[3], r1.at[q], device(z, side, core, member)).start()

    def cut(q, taken):
        for z in range(lines):
            for k in range(4):
                at = z * line_depth + k * depth
                blk[q, z, k] = taken[:, at : at + depth]

    def arrived(ref, recv):
        copy(ref, ref, out.at[0], recv, partner).wait_recv()

    def departed(ref, n):
        copy(ref, ref, out.at[n], rx, partner).wait_send()

    pl.semaphore_wait(barrier, total - 1 + 3)

    swap(0).start()
    loads[3].wait()
    cut(0, dot(pick, tokv[...], ((1,), (0,))).astype(BF16))
    each(1, total, functools.partial(give, 0))
    swap(1).start()
    lend(0).start()
    loads[4].wait()
    cut(1, (dot(pick, cotv[...], ((1,), (0,))) * (slot_weight * active)).astype(BF16))
    swap(2).start()
    each(1, total, functools.partial(give, 1))
    lend(1).start()
    lend(2).start()
    for q in range(2):
        recv1[q, flat] = blk[q, line]

    def product(n, q):
        left = jnp.concatenate([recv1[q, :, k].reshape(total * cap, depth) for k in range(4)], axis=1)
        term = dot(left, wfull[n].reshape(line_depth, width), ((1,), (0,)))
        term = term.reshape(lines, members * cap, width)
        part[n] = term
        send2[n] = term.astype(BF16)
        for d in range(1, lines):
            z, there = on_line(d)
            copy(send2.at[n, z], recv2.at[n, line], out.at[4], r2.at[n], there).start()

    def summed(n):
        arrived(send2.at[n, 1:], r2.at[n])
        total_rows = part[n, line]
        for d in range(1, lines):
            total_rows += recv2[n, on_line(d)[0]].astype(F32)
        return total_rows

    def stage(n, q):
        swap(n).wait_recv()
        relay(n).start()
        if n != 1:
            arrived(recv1.at[q, 1:], r1.at[q])
        arrived(wfull.at[n, 0:2], rwp.at[n])
        product(n, q)

    stage(0, 0)
    stage(1, 0)
    stage(2, 1)

    def share(q, n):
        k, there = beside(n)
        return copy(recv1.at[q, :, k], rows_all.at[q, quarter], out.at[5], rx, there)

    for q in range(2):
        for n in range(3):
            share(q, n).start()
        rows_all[q, quarter] = recv1[q, :, quarter]

    def held(n, z):
        return all3.at[n, quarter, z]

    def spread_out(n):
        for d in range(1, lines):
            _, there = on_line(d)
            copy(held(n, line), held(n, line), out.at[6], r3z.at[n, d - 1], there).start()
        copy(held(n, line), held(n, line), out.at[7], r3y.at[n], across).start()

    def pass_on(n):
        for d in range(1, lines):
            z, there = on_line(d)
            copy(held(n, line), held(n, z), out.at[6], r3z.at[n, d - 1], there).wait_recv()
            copy(held(n, z), held(n, z), out.at[7], r3y.at[n], across).start()
        mine = all3.at[n, quarter]
        copy(mine, mine, out.at[8], r3c.at[n], partner).start()

    def from_across(n):
        arrived(all3.at[n, 0], r3y.at[n])
        theirs = all3.at[n, 2 * (1 - side) + core]
        copy(theirs, theirs, out.at[8], r3c.at[n], partner).start()

    def gradient(n, q, result):
        arrived(all3.at[n, 0:2], r3c.at[n])
        left = rows_all[q].reshape(4 * total * cap, depth)
        result[...] = dot(left, all3[n].reshape(4 * total * cap, width), ((0,), (0,))).astype(BF16)

    gate, up = summed(0), summed(1)
    sig = 1.0 / (1.0 + jnp.exp(-gate))
    all3[0, quarter, line] = (gate * sig * up).astype(BF16)
    spread_out(0)
    dhidden = summed(2)
    all3[1, quarter, line] = (dhidden * up * sig * (1.0 + gate * (1.0 - sig))).astype(BF16)
    spread_out(1)
    all3[2, quarter, line] = (dhidden * gate * sig).astype(BF16)
    spread_out(2)

    pass_on(0)
    hidden = all3[0, quarter].reshape(total * cap, width)
    rows_out = dot(hidden, wfull[2].reshape(line_depth, width), ((1,), (1,)))
    send4[...] = rows_out.astype(BF16).reshape(total, cap, line_depth)

    def return_rows(t):
        z, member = peer(t)
        there = device(z, side, core, member)
        copy(send4.at[z * members + member], recv4.at[j, line], out.at[9], r4, there).start()

    each(1, total, return_rows)
    recv4[j, line] = send4[flat]
    pass_on(1)
    from_across(0)
    pass_on(2)
    arrived(rows_all.at[:, 0:3], rx)
    gradient(0, 1, grad_down)
    from_across(1)
    from_across(2)
    gradient(1, 0, grad_gate)
    arrived(send4.at[1:], r4)
    for z in range(lines):
        out_rows = recv4[0, z].astype(F32)
        for m in range(1, members):
            out_rows += recv4[m, z].astype(F32)
        placed = dot(spread, (out_rows * slot_weight).astype(BF16), ((1,), (0,)))
        mixed[:, z * line_depth : (z + 1) * line_depth] = placed.astype(BF16)
    gradient(2, 0, grad_up)

    for n in range(3):
        departed(wfull.at[:, 0], n)
    departed(recv1.at[:, 1:], 3)
    departed(send2.at[:, 1:], 4)
    departed(rows_all.at[:, 0:3], 5)
    departed(all3.at[:, 0, 1:], 6)
    departed(all3.at[:, 0], 7)
    departed(all3.at[:, 0:2], 8)
    departed(send4.at[1:], 9)


def write_out(*refs):
    sems = refs[-1]
    copies = [pltpu.make_async_copy(refs[n], refs[4 + n], sems.at[n]) for n in range(4)]
    for c in copies:
        c.start()
    for c in copies:
        c.wait()


def per_device(lines, members, tokens, cotangent, expert_ids, route_weights, join_groups, w_gate, w_up, w_down):
    tok_count, model = tokens.shape
    depth, width = w_gate.shape
    cap = tok_count // 8
    total = lines * members
    rows = members * cap
    vmem = pl.BlockSpec(memory_space=pltpu.VMEM)
    hbm = pl.BlockSpec(memory_space=pl.ANY)
    dma = pltpu.SemaphoreType.DMA
    grad = pltpu.VMEM((depth, width), BF16)
    results = pl.pallas_call(
        functools.partial(kernel, lines, members, cap),
        out_shape=(pltpu.VMEM((tok_count, model), BF16), grad, grad, grad),
        in_specs=[hbm] * 8,
        out_specs=(vmem,) * 4,
        scratch_shapes=[
            pltpu.SMEM(join_groups.shape, jnp.int32),
            pltpu.VMEM(expert_ids.shape[::-1], jnp.int32),
            pltpu.VMEM(route_weights.shape[::-1], F32),
            pltpu.VMEM((tok_count, model), BF16),
            pltpu.VMEM((tok_count, model), BF16),
            pltpu.VMEM((3, 4, depth, width), BF16),
            pltpu.VMEM((2, lines, 4, cap, depth), BF16),
            pltpu.VMEM((2, total, 4, cap, depth), BF16),
            pltpu.VMEM((2, 4, total, cap, depth), BF16),
            pltpu.VMEM((3, lines, rows, width), F32),
            pltpu.VMEM((3, lines, rows, width), BF16),
            pltpu.VMEM((3, lines, rows, width), BF16),
            pltpu.VMEM((3, 4, lines, rows, width), BF16),
            pltpu.VMEM((total, cap, 4 * depth), BF16),
            pltpu.VMEM((members, lines, cap, 4 * depth), BF16),
            dma((6,)), dma((10,)),
            dma((3,)), dma((3,)),
            dma((2,)), dma(()),
            dma((3,)),
            dma((3, lines - 1)), dma((3,)), dma((3,)),
            dma(()),
        ],
        compiler_params=pltpu.CompilerParams(
            collective_id=0, has_side_effects=True, vmem_limit_bytes=60 * 1024 * 1024
        ),
        name="expert_step",
    )(join_groups, tokens, cotangent, expert_ids.T, route_weights.T, w_gate, w_up, w_down)
    return pl.pallas_call(
        write_out,
        out_shape=tuple(jax.ShapeDtypeStruct(r.shape, r.dtype) for r in results),
        in_specs=[vmem] * 4,
        out_specs=(hbm,) * 4,
        scratch_shapes=[dma((4,))],
        name="write_out",
    )(*(pltpu.with_memory_space_constraint(r, pltpu.VMEM) for r in results))


def solution(mesh):
    in_specs = (
        P(("dp", "expert"), None),
        P(("dp", "expert"), None),
        P(("dp", "expert"), None),
        P(("dp", "expert"), None),
        P(),
        P("dp", "expert"),
        P("dp", "expert"),
        P("dp", "expert"),
    )
    out_specs = (P(("dp", "expert"), None), P("dp", "expert"), P("dp", "expert"), P("dp", "expert"))
    body = functools.partial(per_device, mesh.shape["dp"] // 4, mesh.shape["expert"])
    return jax.shard_map(body, mesh=mesh, in_specs=in_specs, out_specs=out_specs, check_vma=False)
```

time: 40.6 us -> 39.3 us (0.968)
  Pallas kernels: 39.5 us -> 38.3 us
    pallas_call x1, Pallas kernels: 38.6 us -> 37.3 us  [per_device(): pl.pallas_call(functools.partial(kernel, lines, members, cap), out_shape=...]
where the time goes in v3:
time: 39.3 us; the launch traced here: 38.9 us
  Pallas kernels  38.3 us (97%)
  between operations  0.64 us (2%)
    pallas_call x1, Pallas kernels, per_device(): pl.pallas_call(functools.partial(kernel, lines, members, cap), out_shape=...  37.3 us
    pallas_call x1, Pallas kernels, per_device(): pl.pallas_call(write_out, out_shape=tuple((jax.ShapeDtypeStruct(r.shape,...  0.95 us

profile of v3, /device:TPU:0, one launch (start us, length us, event | category | flops | bytes accessed | tf_op | source)
XLA Modules:
  0.0 38.9 jit_solution(15955886600670970907)
XLA Ops:
  0.6 37.3 %expert_step.1 = (bf16[128,2048]{1,0:T(8,128)(2,1)S(1)}, bf16[128,512]{1,0:T(8,128)(2,1)S(1)}, bf16[128,512]{1,0:T(8,128)(2,1)S(1)}, bf16[128,512]{1,0:T(8,128)(2,1)S(1)}) custom-call(s32[16]{0:T(128)} %join.1, bf16[128,2048]{1,0:T(8,128)(2,1)} %tok.1, bf16[128,2048]{1,0:T(8,128)(2,1)} %cot.1, s32[8,128]{1,0:T(8,128)} %bitcast.2, f32[8,128]{1,0:T(8,128)} %bitcast.3, ...), custom_call_target="tpu_custom_call" | custom-call | tf_op jit(solution)/shard_map/expert_step/pallas_call | solution.py:296
  38.0 1.0 %write_out.1 = (bf16[128,2048]{1,0:T(8,128)(2,1)}, bf16[128,512]{1,0:T(8,128)(2,1)}, bf16[128,512]{1,0:T(8,128)(2,1)}, bf16[128,512]{1,0:T(8,128)(2,1)}) custom-call(bf16[128,2048]{1,0:T(8,128)(2,1)S(1)} %get-tuple-element.8.refs_0_, bf16[128,512]{1,0:T(8,128)(2,1)S(1)} %get-tuple-element.9.refs_1_, bf16[128,512]{1,0:T(8,128)(2,1)S(1)} %get-tuple-element.10.refs_2_, ...), custom_call_target="tpu_custom_call" | custom-call | tf_op jit(solution)/shard_map/write_out/pallas_call | solution.py:329

commit v4 on v3

--- a/solution.py
+++ b/solution.py
@@ -200,16 +200,27 @@
     def held(n, z):
         return all3.at[n, quarter, z]
 
-    def spread_out(n):
-        for d in range(1, lines):
-            _, there = on_line(d)
-            copy(held(n, line), held(n, line), out.at[6], r3z.at[n, d - 1], there).start()
-        copy(held(n, line), held(n, line), out.at[7], r3y.at[n], across).start()
+    last = lines - 1
+    at_end = (line == 0) | (line == last)
+    beside_end = (line == 1) | (line == last - 1)
+
+    def block(n, z, d, sem, there):
+        return copy(held(n, z), held(n, z), sem, r3z.at[n, d - 1], there)
+
+    def spread_out(*which):
+        for d in [last - 1] + list(range(1, last - 1)):
+            for n in which:
+                block(n, line, d, out.at[6], on_line(d)[1]).start()
+        for n in which:
+            pl.when(jnp.logical_not(at_end))(block(n, line, last, out.at[10], on_line(last)[1]).start)
+            copy(held(n, line), held(n, line), out.at[7], r3y.at[n], across).start()
 
     def pass_on(n):
         for d in range(1, lines):
             z, there = on_line(d)
-            copy(held(n, line), held(n, z), out.at[6], r3z.at[n, d - 1], there).wait_recv()
+            block(n, z, d, out.at[6], there).wait_recv()
+            if d == last - 1:
+                pl.when(beside_end)(block(n, z, last, out.at[11], on_line(1)[1]).start)
             copy(held(n, z), held(n, z), out.at[7], r3y.at[n], across).start()
         mine = all3.at[n, quarter]
         copy(mine, mine, out.at[8], r3c.at[n], partner).start()
@@ -230,9 +241,8 @@
     spread_out(0)
     dhidden = summed(2)
     all3[1, quarter, line] = (dhidden * up * sig * (1.0 + gate * (1.0 - sig))).astype(BF16)
-    spread_out(1)
     all3[2, quarter, line] = (dhidden * gate * sig).astype(BF16)
-    spread_out(2)
+    spread_out(1, 2)
 
     pass_on(0)
     hidden = all3[0, quarter].reshape(total * cap, width)
@@ -268,7 +278,9 @@
     departed(recv1.at[:, 1:], 3)
     departed(send2.at[:, 1:], 4)
     departed(rows_all.at[:, 0:3], 5)
-    departed(all3.at[:, 0, 1:], 6)
+    departed(all3.at[:, 0, 1:last], 6)
+    pl.when(jnp.logical_not(at_end))(functools.partial(departed, all3.at[:, 0, 0], 10))
+    pl.when(beside_end)(functools.partial(departed, all3.at[:, 0, 0], 11))
     departed(all3.at[:, 0], 7)
     departed(all3.at[:, 0:2], 8)
     departed(send4.at[1:], 9)
@@ -314,7 +326,7 @@
             pltpu.VMEM((3, 4, lines, rows, width), BF16),
             pltpu.VMEM((total, cap, 4 * depth), BF16),
             pltpu.VMEM((members, lines, cap, 4 * depth), BF16),
-            dma((6,)), dma((10,)),
+            dma((6,)), dma((12,)),
             dma((3,)), dma((3,)),
             dma((2,)), dma(()),
             dma((3,)),

time: 39.3 us -> 38.5 us (0.980)
  Pallas kernels: 38.3 us -> 37.7 us
    pallas_call x1, Pallas kernels: 37.3 us -> 36.8 us  [per_device(): pl.pallas_call(functools.partial(kernel, lines, members, cap), out_shape=...]
where the time goes in v4:
time: 38.5 us; the launch traced here: 38.3 us
  Pallas kernels  37.7 us (98%)
  between operations  0.64 us (2%)
    pallas_call x1, Pallas kernels, per_device(): pl.pallas_call(functools.partial(kernel, lines, members, cap), out_shape=...  36.8 us
    pallas_call x1, Pallas kernels, per_device(): pl.pallas_call(write_out, out_shape=tuple((jax.ShapeDtypeStruct(r.shape,...  0.95 us

profile of v4, /device:TPU:0, one launch (start us, length us, event | category | flops | bytes accessed | tf_op | source)
XLA Modules:
  0.0 38.3 jit_solution(12129916543285844073)
XLA Ops:
  0.6 36.8 %expert_step.1 = (bf16[128,2048]{1,0:T(8,128)(2,1)S(1)}, bf16[128,512]{1,0:T(8,128)(2,1)S(1)}, bf16[128,512]{1,0:T(8,128)(2,1)S(1)}, bf16[128,512]{1,0:T(8,128)(2,1)S(1)}) custom-call(s32[16]{0:T(128)} %join.1, bf16[128,2048]{1,0:T(8,128)(2,1)} %tok.1, bf16[128,2048]{1,0:T(8,128)(2,1)} %cot.1, s32[8,128]{1,0:T(8,128)} %bitcast.2, f32[8,128]{1,0:T(8,128)} %bitcast.3, ...), custom_call_target="tpu_custom_call" | custom-call | tf_op jit(solution)/shard_map/expert_step/pallas_call | solution.py:308
  37.4 1.0 %write_out.1 = (bf16[128,2048]{1,0:T(8,128)(2,1)}, bf16[128,512]{1,0:T(8,128)(2,1)}, bf16[128,512]{1,0:T(8,128)(2,1)}, bf16[128,512]{1,0:T(8,128)(2,1)}) custom-call(bf16[128,2048]{1,0:T(8,128)(2,1)S(1)} %get-tuple-element.8.refs_0_, bf16[128,512]{1,0:T(8,128)(2,1)S(1)} %get-tuple-element.9.refs_1_, bf16[128,512]{1,0:T(8,128)(2,1)S(1)} %get-tuple-element.10.refs_2_, ...), custom_call_target="tpu_custom_call" | custom-call | tf_op jit(solution)/shard_map/write_out/pallas_call | solution.py:341

commit v5 on v4

--- a/solution.py
+++ b/solution.py
@@ -78,6 +78,7 @@
         c = 1 - core if near[n][1] else core
         return 2 * y + c, device(line, y, c, j)
 
+    slanted = device(flip(line, 1, lines), 1 - side, core, j)
     barrier = pltpu.get_barrier_semaphore()
 
     def greet(t):
@@ -85,8 +86,8 @@
         pl.semaphore_signal(barrier, inc=1, device_id=device(z, side, core, member), device_id_type=MESH)
 
     each(1, total, greet)
-    for n in range(3):
-        pl.semaphore_signal(barrier, inc=1, device_id=beside(n)[1], device_id_type=MESH)
+    for there in [beside(n)[1] for n in range(3)] + [slanted]:
+        pl.semaphore_signal(barrier, inc=1, device_id=there, device_id_type=MESH)
 
     loads = [
         pltpu.make_async_copy(src, dst, local.at[n])
@@ -142,7 +143,7 @@
     def departed(ref, n):
         copy(ref, ref, out.at[n], rx, partner).wait_send()
 
-    pl.semaphore_wait(barrier, total - 1 + 3)
+    pl.semaphore_wait(barrier, total - 1 + 4)
 
     swap(0).start()
     loads[3].wait()
@@ -215,13 +216,25 @@
             pl.when(jnp.logical_not(at_end))(block(n, line, last, out.at[10], on_line(last)[1]).start)
             copy(held(n, line), held(n, line), out.at[7], r3y.at[n], across).start()
 
-    def pass_on(n):
-        for d in range(1, lines):
-            z, there = on_line(d)
-            block(n, z, d, out.at[6], there).wait_recv()
-            if d == last - 1:
-                pl.when(beside_end)(block(n, z, last, out.at[11], on_line(1)[1]).start)
-            copy(held(n, z), held(n, z), out.at[7], r3y.at[n], across).start()
+    def across_with(n, z, sem, there):
+        return copy(held(n, z), held(n, z), sem, r3y.at[n], there)
+
+    def take_in(n, d):
+        z, there = on_line(d)
+        block(n, z, d, out.at[6], there).wait_recv()
+        if d == last - 1:
+
+            @pl.when(beside_end)
+            def _():
+                block(n, z, last, out.at[11], on_line(1)[1]).start()
+                across_with(n, z, out.at[12], slanted).start()
+
+        if d == last:
+            pl.when(jnp.logical_not(at_end))(across_with(n, z, out.at[13], across).start)
+        else:
+            across_with(n, z, out.at[7], across).start()
+
+    def to_partner(n):
         mine = all3.at[n, quarter]
         copy(mine, mine, out.at[8], r3c.at[n], partner).start()
 
@@ -244,24 +257,40 @@
     all3[2, quarter, line] = (dhidden * gate * sig).astype(BF16)
     spread_out(1, 2)
 
-    pass_on(0)
-    hidden = all3[0, quarter].reshape(total * cap, width)
-    rows_out = dot(hidden, wfull[2].reshape(line_depth, width), ((1,), (1,)))
-    send4[...] = rows_out.astype(BF16).reshape(total, cap, line_depth)
-
-    def return_rows(t):
-        z, member = peer(t)
-        there = device(z, side, core, member)
-        copy(send4.at[z * members + member], recv4.at[j, line], out.at[9], r4, there).start()
-
-    each(1, total, return_rows)
+    def rows_out(steps):
+        places = [flip(line, d, lines) for d in steps]
+        hidden = jnp.concatenate([all3[0, quarter, z] for z in places], axis=0)
+        rows = dot(hidden, wfull[2].reshape(line_depth, width), ((1,), (1,))).astype(BF16)
+        rows = rows.reshape(len(places), members, cap, line_depth)
+        for i, (d, z) in enumerate(zip(steps, places)):
+            for m in range(members):
+                send4[z * members + m] = rows[i, m]
+
+            def send(dj, d=d, z=z):
+                member = flip(j, dj, members)
+                there = device(z, side, core, member)
+                copy(send4.at[z * members + member], recv4.at[j, line], out.at[9], r4, there).start()
+
+            for dj in range(0 if d else 1, members):
+                send(dj)
+
+    for d in range(1, last):
+        take_in(0, d)
+    rows_out(list(range(last)))
+    for d in range(1, last):
+        take_in(1, d)
+        take_in(2, d)
+    take_in(0, last)
+    to_partner(0)
+    rows_out([last])
     recv4[j, line] = send4[flat]
-    pass_on(1)
+    for n in (1, 2):
+        take_in(n, last)
+        to_partner(n)
     from_across(0)
-    pass_on(2)
+    from_across(1)
     arrived(rows_all.at[:, 0:3], rx)
     gradient(0, 1, grad_down)
-    from_across(1)
     from_across(2)
     gradient(1, 0, grad_gate)
     arrived(send4.at[1:], r4)
@@ -280,8 +309,10 @@
     departed(rows_all.at[:, 0:3], 5)
     departed(all3.at[:, 0, 1:last], 6)
     pl.when(jnp.logical_not(at_end))(functools.partial(departed, all3.at[:, 0, 0], 10))
+    pl.when(jnp.logical_not(at_end))(functools.partial(departed, all3.at[:, 0, 0], 13))
     pl.when(beside_end)(functools.partial(departed, all3.at[:, 0, 0], 11))
-    departed(all3.at[:, 0], 7)
+    pl.when(beside_end)(functools.partial(departed, all3.at[:, 0, 0], 12))
+    departed(all3.at[:, 0, 0:last], 7)
     departed(all3.at[:, 0:2], 8)
     departed(send4.at[1:], 9)
 
@@ -326,7 +357,7 @@
             pltpu.VMEM((3, 4, lines, rows, width), BF16),
             pltpu.VMEM((total, cap, 4 * depth), BF16),
             pltpu.VMEM((members, lines, cap, 4 * depth), BF16),
-            dma((6,)), dma((12,)),
+            dma((6,)), dma((14,)),
             dma((3,)), dma((3,)),
             dma((2,)), dma(()),
             dma((3,)),

time: 38.5 us -> 38.1 us (0.990)
  Pallas kernels: 37.7 us -> 37.3 us
    pallas_call x1, Pallas kernels: 36.8 us -> 36.3 us  [per_device(): pl.pallas_call(functools.partial(kernel, lines, members, cap), out_shape=...]
where the time goes in v5:
time: 38.1 us; the launch traced here: 37.9 us
  Pallas kernels  37.3 us (98%)
  between operations  0.64 us (2%)
    pallas_call x1, Pallas kernels, per_device(): pl.pallas_call(functools.partial(kernel, lines, members, cap), out_shape=...  36.3 us
    pallas_call x1, Pallas kernels, per_device(): pl.pallas_call(write_out, out_shape=tuple((jax.ShapeDtypeStruct(r.shape,...  0.95 us

profile of v5, /device:TPU:0, one launch (start us, length us, event | category | flops | bytes accessed | tf_op | source)
XLA Modules:
  0.0 37.9 jit_solution(15573323746671565441)
XLA Ops:
  0.6 36.3 %expert_step.1 = (bf16[128,2048]{1,0:T(8,128)(2,1)S(1)}, bf16[128,512]{1,0:T(8,128)(2,1)S(1)}, bf16[128,512]{1,0:T(8,128)(2,1)S(1)}, bf16[128,512]{1,0:T(8,128)(2,1)S(1)}) custom-call(s32[16]{0:T(128)} %join.1, bf16[128,2048]{1,0:T(8,128)(2,1)} %tok.1, bf16[128,2048]{1,0:T(8,128)(2,1)} %cot.1, s32[8,128]{1,0:T(8,128)} %bitcast.2, f32[8,128]{1,0:T(8,128)} %bitcast.3, ...), custom_call_target="tpu_custom_call" | custom-call | tf_op jit(solution)/shard_map/expert_step/pallas_call | solution.py:339
  37.0 1.0 %write_out.1 = (bf16[128,2048]{1,0:T(8,128)(2,1)}, bf16[128,512]{1,0:T(8,128)(2,1)}, bf16[128,512]{1,0:T(8,128)(2,1)}, bf16[128,512]{1,0:T(8,128)(2,1)}) custom-call(bf16[128,2048]{1,0:T(8,128)(2,1)S(1)} %get-tuple-element.8.refs_0_, bf16[128,512]{1,0:T(8,128)(2,1)S(1)} %get-tuple-element.9.refs_1_, bf16[128,512]{1,0:T(8,128)(2,1)S(1)} %get-tuple-element.10.refs_2_, ...), custom_call_target="tpu_custom_call" | custom-call | tf_op jit(solution)/shard_map/write_out/pallas_call | solution.py:372

commit v6 on v5

--- a/solution.py
+++ b/solution.py
@@ -276,13 +276,12 @@
 
     for d in range(1, last):
         take_in(0, d)
-    rows_out(list(range(last)))
     for d in range(1, last):
         take_in(1, d)
         take_in(2, d)
     take_in(0, last)
     to_partner(0)
-    rows_out([last])
+    rows_out(list(range(lines)))
     recv4[j, line] = send4[flat]
     for n in (1, 2):
         take_in(n, last)

time: 38.1 us -> 38 us (level)
  no operation moved by 1% of the time
where the time goes in v6:
time: 38 us; the launch traced here: 37.8 us
  Pallas kernels  37.1 us (98%)
  between operations  0.64 us (2%)
    pallas_call x1, Pallas kernels, per_device(): pl.pallas_call(functools.partial(kernel, lines, members, cap), out_shape=...  36.2 us
    pallas_call x1, Pallas kernels, per_device(): pl.pallas_call(write_out, out_shape=tuple((jax.ShapeDtypeStruct(r.shape,...  0.95 us

profile of v6, /device:TPU:0, one launch (start us, length us, event | category | flops | bytes accessed | tf_op | source)
XLA Modules:
  0.0 37.8 jit_solution(11982938145678054915)
XLA Ops:
  0.6 36.2 %expert_step.1 = (bf16[128,2048]{1,0:T(8,128)(2,1)S(1)}, bf16[128,512]{1,0:T(8,128)(2,1)S(1)}, bf16[128,512]{1,0:T(8,128)(2,1)S(1)}, bf16[128,512]{1,0:T(8,128)(2,1)S(1)}) custom-call(s32[16]{0:T(128)} %join.1, bf16[128,2048]{1,0:T(8,128)(2,1)} %tok.1, bf16[128,2048]{1,0:T(8,128)(2,1)} %cot.1, s32[8,128]{1,0:T(8,128)} %bitcast.2, f32[8,128]{1,0:T(8,128)} %bitcast.3, ...), custom_call_target="tpu_custom_call" | custom-call | tf_op jit(solution)/shard_map/expert_step/pallas_call | solution.py:338
  36.8 1.0 %write_out.1 = (bf16[128,2048]{1,0:T(8,128)(2,1)}, bf16[128,512]{1,0:T(8,128)(2,1)}, bf16[128,512]{1,0:T(8,128)(2,1)}, bf16[128,512]{1,0:T(8,128)(2,1)}) custom-call(bf16[128,2048]{1,0:T(8,128)(2,1)S(1)} %get-tuple-element.8.refs_0_, bf16[128,512]{1,0:T(8,128)(2,1)S(1)} %get-tuple-element.9.refs_1_, bf16[128,512]{1,0:T(8,128)(2,1)S(1)} %get-tuple-element.10.refs_2_, ...), custom_call_target="tpu_custom_call" | custom-call | tf_op jit(solution)/shard_map/write_out/pallas_call | solution.py:371

commit v7 on v6

--- a/solution.py
+++ b/solution.py
@@ -9,6 +9,7 @@
 
 F32, BF16 = jnp.float32, jnp.bfloat16
 MESH = pl.DeviceIdType.MESH
+RELAYED, SLANTED = (0, 2), (2,)
 
 
 def dot(a, b, dims):
@@ -213,7 +214,10 @@
             for n in which:
                 block(n, line, d, out.at[6], on_line(d)[1]).start()
         for n in which:
-            pl.when(jnp.logical_not(at_end))(block(n, line, last, out.at[10], on_line(last)[1]).start)
+            if n in RELAYED:
+                pl.when(jnp.logical_not(at_end))(block(n, line, last, out.at[10], on_line(last)[1]).start)
+            else:
+                block(n, line, last, out.at[14], on_line(last)[1]).start()
             copy(held(n, line), held(n, line), out.at[7], r3y.at[n], across).start()
 
     def across_with(n, z, sem, there):
@@ -222,17 +226,14 @@
     def take_in(n, d):
         z, there = on_line(d)
         block(n, z, d, out.at[6], there).wait_recv()
-        if d == last - 1:
-
-            @pl.when(beside_end)
-            def _():
-                block(n, z, last, out.at[11], on_line(1)[1]).start()
-                across_with(n, z, out.at[12], slanted).start()
-
-        if d == last:
+        if d == last - 1 and n in RELAYED:
+            pl.when(beside_end)(block(n, z, last, out.at[11], on_line(1)[1]).start)
+            if n in SLANTED:
+                pl.when(beside_end)(across_with(n, z, out.at[12], slanted).start)
+        if d == last and n in SLANTED:
             pl.when(jnp.logical_not(at_end))(across_with(n, z, out.at[13], across).start)
         else:
-            across_with(n, z, out.at[7], across).start()
+            across_with(n, z, out.at[7 if d < last else 15], across).start()
 
     def to_partner(n):
         mine = all3.at[n, quarter]
@@ -307,10 +308,14 @@
     departed(send2.at[:, 1:], 4)
     departed(rows_all.at[:, 0:3], 5)
     departed(all3.at[:, 0, 1:last], 6)
-    pl.when(jnp.logical_not(at_end))(functools.partial(departed, all3.at[:, 0, 0], 10))
-    pl.when(jnp.logical_not(at_end))(functools.partial(departed, all3.at[:, 0, 0], 13))
-    pl.when(beside_end)(functools.partial(departed, all3.at[:, 0, 0], 11))
-    pl.when(beside_end)(functools.partial(departed, all3.at[:, 0, 0], 12))
+    inner = jnp.logical_not(at_end)
+    for n, count, who in (
+        (10, len(RELAYED), inner), (11, len(RELAYED), beside_end), (12, len(SLANTED), beside_end),
+        (13, len(SLANTED), inner), (14, 3 - len(RELAYED), None), (15, 3 - len(SLANTED), None),
+    ):
+        if count:
+            finish = functools.partial(departed, all3.at[0:count, 0, 0], n)
+            finish() if who is None else pl.when(who)(finish)
     departed(all3.at[:, 0, 0:last], 7)
     departed(all3.at[:, 0:2], 8)
     departed(send4.at[1:], 9)
@@ -356,7 +361,7 @@
             pltpu.VMEM((3, 4, lines, rows, width), BF16),
             pltpu.VMEM((total, cap, 4 * depth), BF16),
             pltpu.VMEM((members, lines, cap, 4 * depth), BF16),
-            dma((6,)), dma((14,)),
+            dma((6,)), dma((16,)),
             dma((3,)), dma((3,)),
             dma((2,)), dma(()),
             dma((3,)),

time: 38 us -> 38.4 us (1.011)
  Pallas kernels: 37.1 us -> 37.5 us
    pallas_call x1, Pallas kernels: 36.2 us -> 36.6 us  [per_device(): pl.pallas_call(functools.partial(kernel, lines, members, cap), out_shape=...]
where the time goes in v7:
time: 38.4 us; the launch traced here: 38.2 us
  Pallas kernels  37.5 us (98%)
  between operations  0.64 us (2%)
    pallas_call x1, Pallas kernels, per_device(): pl.pallas_call(functools.partial(kernel, lines, members, cap), out_shape=...  36.6 us
    pallas_call x1, Pallas kernels, per_device(): pl.pallas_call(write_out, out_shape=tuple((jax.ShapeDtypeStruct(r.shape,...  0.95 us

profile of v7, /device:TPU:0, one launch (start us, length us, event | category | flops | bytes accessed | tf_op | source)
XLA Modules:
  0.0 38.2 jit_solution(7355912139119492995)
XLA Ops:
  0.6 36.6 %expert_step.1 = (bf16[128,2048]{1,0:T(8,128)(2,1)S(1)}, bf16[128,512]{1,0:T(8,128)(2,1)S(1)}, bf16[128,512]{1,0:T(8,128)(2,1)S(1)}, bf16[128,512]{1,0:T(8,128)(2,1)S(1)}) custom-call(s32[16]{0:T(128)} %join.1, bf16[128,2048]{1,0:T(8,128)(2,1)} %tok.1, bf16[128,2048]{1,0:T(8,128)(2,1)} %cot.1, s32[8,128]{1,0:T(8,128)} %bitcast.2, f32[8,128]{1,0:T(8,128)} %bitcast.3, ...), custom_call_target="tpu_custom_call" | custom-call | tf_op jit(solution)/shard_map/expert_step/pallas_call | solution.py:343
  37.2 1.0 %write_out.1 = (bf16[128,2048]{1,0:T(8,128)(2,1)}, bf16[128,512]{1,0:T(8,128)(2,1)}, bf16[128,512]{1,0:T(8,128)(2,1)}, bf16[128,512]{1,0:T(8,128)(2,1)}) custom-call(bf16[128,2048]{1,0:T(8,128)(2,1)S(1)} %get-tuple-element.8.refs_0_, bf16[128,512]{1,0:T(8,128)(2,1)S(1)} %get-tuple-element.9.refs_1_, bf16[128,512]{1,0:T(8,128)(2,1)S(1)} %get-tuple-element.10.refs_2_, ...), custom_call_target="tpu_custom_call" | custom-call | tf_op jit(solution)/shard_map/write_out/pallas_call | solution.py:376

commit v8 on v4

--- a/solution.py
+++ b/solution.py
@@ -85,8 +85,8 @@
         pl.semaphore_signal(barrier, inc=1, device_id=device(z, side, core, member), device_id_type=MESH)
 
     each(1, total, greet)
-    for n in range(3):
-        pl.semaphore_signal(barrier, inc=1, device_id=beside(n)[1], device_id_type=MESH)
+    for there in [beside(n)[1] for n in range(3)]:
+        pl.semaphore_signal(barrier, inc=1, device_id=there, device_id_type=MESH)
 
     loads = [
         pltpu.make_async_copy(src, dst, local.at[n])
@@ -202,6 +202,7 @@
 
     last = lines - 1
     at_end = (line == 0) | (line == last)
+    inner = jnp.logical_not(at_end)
     beside_end = (line == 1) | (line == last - 1)
 
     def block(n, z, d, sem, there):
@@ -212,16 +213,17 @@
             for n in which:
                 block(n, line, d, out.at[6], on_line(d)[1]).start()
         for n in which:
-            pl.when(jnp.logical_not(at_end))(block(n, line, last, out.at[10], on_line(last)[1]).start)
+            pl.when(inner)(block(n, line, last, out.at[10], on_line(last)[1]).start)
             copy(held(n, line), held(n, line), out.at[7], r3y.at[n], across).start()
 
-    def pass_on(n):
-        for d in range(1, lines):
-            z, there = on_line(d)
-            block(n, z, d, out.at[6], there).wait_recv()
-            if d == last - 1:
-                pl.when(beside_end)(block(n, z, last, out.at[11], on_line(1)[1]).start)
-            copy(held(n, z), held(n, z), out.at[7], r3y.at[n], across).start()
+    def take_in(n, d):
+        z, there = on_line(d)
+        block(n, z, d, out.at[6], there).wait_recv()
+        if d == last - 1:
+            pl.when(beside_end)(block(n, z, last, out.at[11], on_line(1)[1]).start)
+        copy(held(n, z), held(n, z), out.at[7], r3y.at[n], across).start()
+
+    def to_partner(n):
         mine = all3.at[n, quarter]
         copy(mine, mine, out.at[8], r3c.at[n], partner).start()
 
@@ -244,24 +246,56 @@
     all3[2, quarter, line] = (dhidden * gate * sig).astype(BF16)
     spread_out(1, 2)
 
-    pass_on(0)
-    hidden = all3[0, quarter].reshape(total * cap, width)
-    rows_out = dot(hidden, wfull[2].reshape(line_depth, width), ((1,), (1,)))
-    send4[...] = rows_out.astype(BF16).reshape(total, cap, line_depth)
-
-    def return_rows(t):
-        z, member = peer(t)
-        there = device(z, side, core, member)
-        copy(send4.at[z * members + member], recv4.at[j, line], out.at[9], r4, there).start()
-
-    each(1, total, return_rows)
-    recv4[j, line] = send4[flat]
-    pass_on(1)
+    def finish(n):
+        take_in(n, last)
+        to_partner(n)
+
+    def output_rows():
+        places = [flip(line, d, lines) for d in range(lines)]
+        hidden = jnp.concatenate([all3[0, quarter, z] for z in places], axis=0)
+        rows = dot(hidden, wfull[2].reshape(line_depth, width), ((1,), (1,))).astype(BF16)
+        rows = rows.reshape(lines, members, cap, line_depth)
+        for i, z in enumerate(places):
+            for m in range(members):
+                send4[z * members + m] = rows[i, m]
+            for dj in range(0 if i else 1, members):
+                member = flip(j, dj, members)
+                there = device(z, side, core, member)
+                copy(send4.at[z * members + member], recv4.at[j, line], out.at[9], r4, there).start()
+        recv4[j, line] = send4[flat]
+
+    far = last - 1
+
+    @pl.when(at_end)
+    def _():
+        for d in range(1, far + 1):
+            take_in(0, d)
+        for d in range(1, far):
+            take_in(1, d)
+            take_in(2, d)
+        finish(0)
+        output_rows()
+        take_in(1, far)
+        take_in(2, far)
+        finish(1)
+        finish(2)
+
+    @pl.when(inner)
+    def _():
+        for d in range(1, last):
+            take_in(0, d)
+        finish(0)
+        for d in range(1, last):
+            take_in(1, d)
+            take_in(2, d)
+        output_rows()
+        finish(1)
+        finish(2)
+
     from_across(0)
-    pass_on(2)
+    from_across(1)
     arrived(rows_all.at[:, 0:3], rx)
     gradient(0, 1, grad_down)
-    from_across(1)
     from_across(2)
     gradient(1, 0, grad_gate)
     arrived(send4.at[1:], r4)
@@ -279,7 +313,7 @@
     departed(send2.at[:, 1:], 4)
     departed(rows_all.at[:, 0:3], 5)
     departed(all3.at[:, 0, 1:last], 6)
-    pl.when(jnp.logical_not(at_end))(functools.partial(departed, all3.at[:, 0, 0], 10))
+    pl.when(inner)(functools.partial(departed, all3.at[:, 0, 0], 10))
     pl.when(beside_end)(functools.partial(departed, all3.at[:, 0, 0], 11))
     departed(all3.at[:, 0], 7)
     departed(all3.at[:, 0:2], 8)

time: 38.5 us -> 37.1 us (0.964)
  Pallas kernels: 37.7 us -> 36.3 us
    pallas_call x1, Pallas kernels: 36.8 us -> 35.3 us  [per_device(): pl.pallas_call(functools.partial(kernel, lines, members, cap), out_shape=...]
where the time goes in v8:
time: 37.1 us; the launch traced here: 36.9 us
  Pallas kernels  36.3 us (98%)
  between operations  0.64 us (2%)
    pallas_call x1, Pallas kernels, per_device(): pl.pallas_call(functools.partial(kernel, lines, members, cap), out_shape=...  35.3 us
    pallas_call x1, Pallas kernels, per_device(): pl.pallas_call(write_out, out_shape=tuple((jax.ShapeDtypeStruct(r.shape,...  0.95 us

profile of v8, /device:TPU:0, one launch (start us, length us, event | category | flops | bytes accessed | tf_op | source)
XLA Modules:
  0.0 36.9 jit_solution(15159369153007489306)
XLA Ops:
  0.6 35.3 %expert_step.1 = (bf16[128,2048]{1,0:T(8,128)(2,1)S(1)}, bf16[128,512]{1,0:T(8,128)(2,1)S(1)}, bf16[128,512]{1,0:T(8,128)(2,1)S(1)}, bf16[128,512]{1,0:T(8,128)(2,1)S(1)}) custom-call(s32[16]{0:T(128)} %join.1, bf16[128,2048]{1,0:T(8,128)(2,1)} %tok.1, bf16[128,2048]{1,0:T(8,128)(2,1)} %cot.1, s32[8,128]{1,0:T(8,128)} %bitcast.2, f32[8,128]{1,0:T(8,128)} %bitcast.3, ...), custom_call_target="tpu_custom_call" | custom-call | tf_op jit(solution)/shard_map/expert_step/pallas_call | solution.py:342
  36.0 1.0 %write_out.1 = (bf16[128,2048]{1,0:T(8,128)(2,1)}, bf16[128,512]{1,0:T(8,128)(2,1)}, bf16[128,512]{1,0:T(8,128)(2,1)}, bf16[128,512]{1,0:T(8,128)(2,1)}) custom-call(bf16[128,2048]{1,0:T(8,128)(2,1)S(1)} %get-tuple-element.8.refs_0_, bf16[128,512]{1,0:T(8,128)(2,1)S(1)} %get-tuple-element.9.refs_1_, bf16[128,512]{1,0:T(8,128)(2,1)S(1)} %get-tuple-element.10.refs_2_, ...), custom_call_target="tpu_custom_call" | custom-call | tf_op jit(solution)/shard_map/write_out/pallas_call | solution.py:375

commit v9 on v8

--- a/solution.py
+++ b/solution.py
@@ -9,6 +9,7 @@
 
 F32, BF16 = jnp.float32, jnp.bfloat16
 MESH = pl.DeviceIdType.MESH
+SPLIT = (1, 1, 2)
 
 
 def dot(a, b, dims):
@@ -37,7 +38,7 @@
     lines, members, cap,
     join, tok, cot, ids, wts, wg, wu, wd,
     mixed, grad_gate, grad_up, grad_down,
-    joinv, idv, wtv, tokv, cotv, wfull, blk, recv1, rows_all, part, send2, recv2, all3, send4, recv4,
+    joinv, idv, wtv, tokv, cotv, wfull, blk, recv1, rows_all, part, send2, recv2, all3, half_sum, send4, recv4,
     local, out, rwy, rwp, r1, rx, r2, r3z, r3y, r3c, r4,
 ):
     p, j = lax.axis_index("dp"), lax.axis_index("expert")
@@ -165,15 +166,23 @@
         term = term.reshape(lines, members * cap, width)
         part[n] = term
         send2[n] = term.astype(BF16)
+        for e in range(SPLIT[n]):
+            span = band(n, e)
+            for d in range(1, lines):
+                z, there = on_line(d)
+                recv = r2.at[n + e]
+                copy(send2.at[n, z, span], recv2.at[n, line, span], out.at[4], recv, there).start()
+
+    def band(n, e):
+        height = members * cap // SPLIT[n]
+        return slice(e * height, (e + 1) * height)
+
+    def summed(n, e=0):
+        span = band(n, e)
+        arrived(send2.at[n, 1:, span], r2.at[n + e])
+        total_rows = part[n, line, span]
         for d in range(1, lines):
-            z, there = on_line(d)
-            copy(send2.at[n, z], recv2.at[n, line], out.at[4], r2.at[n], there).start()
-
-    def summed(n):
-        arrived(send2.at[n, 1:], r2.at[n])
-        total_rows = part[n, line]
-        for d in range(1, lines):
-            total_rows += recv2[n, on_line(d)[0]].astype(F32)
+            total_rows += recv2[n, on_line(d)[0], span].astype(F32)
         return total_rows
 
     def stage(n, q):
@@ -197,8 +206,11 @@
             share(q, n).start()
         rows_all[q, quarter] = recv1[q, :, quarter]
 
+    def unit(n, *place):
+        return all3.at[(0, *place)] if n == 0 else all3.at[(slice(1, 3), *place, band(2, n - 1))]
+
     def held(n, z):
-        return all3.at[n, quarter, z]
+        return unit(n, quarter, z)
 
     last = lines - 1
     at_end = (line == 0) | (line == last)
@@ -224,27 +236,33 @@
         copy(held(n, z), held(n, z), out.at[7], r3y.at[n], across).start()
 
     def to_partner(n):
-        mine = all3.at[n, quarter]
+        mine = unit(n, quarter, slice(None)) if n else unit(0, quarter)
         copy(mine, mine, out.at[8], r3c.at[n], partner).start()
 
     def from_across(n):
         arrived(all3.at[n, 0], r3y.at[n])
-        theirs = all3.at[n, 2 * (1 - side) + core]
+        other = 2 * (1 - side) + core
+        theirs = unit(n, other, slice(None)) if n else unit(0, other)
         copy(theirs, theirs, out.at[8], r3c.at[n], partner).start()
 
-    def gradient(n, q, result):
-        arrived(all3.at[n, 0:2], r3c.at[n])
-        left = rows_all[q].reshape(4 * total * cap, depth)
-        result[...] = dot(left, all3[n].reshape(4 * total * cap, width), ((0,), (0,))).astype(BF16)
+    def gradient(n, q, e, parts):
+        height = members * cap // parts
+        span = slice(e * height, (e + 1) * height)
+        left = rows_all[q].reshape(4, lines, members * cap, depth)[:, :, span]
+        right = all3[n, :, :, span]
+        count = 4 * lines * height
+        return dot(left.reshape(count, depth), right.reshape(count, width), ((0,), (0,)))
 
     gate, up = summed(0), summed(1)
     sig = 1.0 / (1.0 + jnp.exp(-gate))
     all3[0, quarter, line] = (gate * sig * up).astype(BF16)
     spread_out(0)
-    dhidden = summed(2)
-    all3[1, quarter, line] = (dhidden * up * sig * (1.0 + gate * (1.0 - sig))).astype(BF16)
-    all3[2, quarter, line] = (dhidden * gate * sig).astype(BF16)
-    spread_out(1, 2)
+    to_gate, to_up = up * sig * (1.0 + gate * (1.0 - sig)), gate * sig
+    for e in range(2):
+        dhidden, span = summed(2, e), band(2, e)
+        all3[1, quarter, line, span] = (dhidden * to_gate[span]).astype(BF16)
+        all3[2, quarter, line, span] = (dhidden * to_up[span]).astype(BF16)
+        spread_out(1 + e)
 
     def finish(n):
         take_in(n, last)
@@ -295,9 +313,12 @@
     from_across(0)
     from_across(1)
     arrived(rows_all.at[:, 0:3], rx)
-    gradient(0, 1, grad_down)
+    arrived(all3.at[0, 0:2], r3c.at[0])
+    grad_down[...] = gradient(0, 1, 0, 1).astype(BF16)
+    arrived(all3.at[0, 0:2], r3c.at[1])
+    for n in range(2):
+        half_sum[n] = gradient(1 + n, 0, 0, 2)
     from_across(2)
-    gradient(1, 0, grad_gate)
     arrived(send4.at[1:], r4)
     for z in range(lines):
         out_rows = recv4[0, z].astype(F32)
@@ -305,7 +326,9 @@
             out_rows += recv4[m, z].astype(F32)
         placed = dot(spread, (out_rows * slot_weight).astype(BF16), ((1,), (0,)))
         mixed[:, z * line_depth : (z + 1) * line_depth] = placed.astype(BF16)
-    gradient(2, 0, grad_up)
+    arrived(all3.at[0, 0:2], r3c.at[2])
+    for n, result in enumerate((grad_gate, grad_up)):
+        result[...] = (half_sum[n] + gradient(1 + n, 0, 1, 2)).astype(BF16)
 
     for n in range(3):
         departed(wfull.at[:, 0], n)
@@ -358,12 +381,13 @@
             pltpu.VMEM((3, lines, rows, width), BF16),
             pltpu.VMEM((3, lines, rows, width), BF16),
             pltpu.VMEM((3, 4, lines, rows, width), BF16),
+            pltpu.VMEM((2, depth, width), F32),
             pltpu.VMEM((total, cap, 4 * depth), BF16),
             pltpu.VMEM((members, lines, cap, 4 * depth), BF16),
             dma((6,)), dma((12,)),
             dma((3,)), dma((3,)),
             dma((2,)), dma(()),
-            dma((3,)),
+            dma((4,)),
             dma((3, lines - 1)), dma((3,)), dma((3,)),
             dma(()),
         ],

time: 37.1 us -> 37.9 us (1.022)
  Pallas kernels: 36.3 us -> 37.1 us
    pallas_call x1, Pallas kernels: 35.3 us -> 36.1 us  [per_device(): pl.pallas_call(functools.partial(kernel, lines, members, cap), out_shape=...]
where the time goes in v9:
time: 37.9 us; the launch traced here: 37.7 us
  Pallas kernels  37.1 us (98%)
  between operations  0.64 us (2%)
    pallas_call x1, Pallas kernels, per_device(): pl.pallas_call(functools.partial(kernel, lines, members, cap), out_shape=...  36.1 us
    pallas_call x1, Pallas kernels, per_device(): pl.pallas_call(write_out, out_shape=tuple((jax.ShapeDtypeStruct(r.shape,...  0.95 us

profile of v9, /device:TPU:0, one launch (start us, length us, event | category | flops | bytes accessed | tf_op | source)
XLA Modules:
  0.0 37.7 jit_solution(17459978192092955132)
XLA Ops:
  0.6 36.1 %expert_step.1 = (bf16[128,2048]{1,0:T(8,128)(2,1)S(1)}, bf16[128,512]{1,0:T(8,128)(2,1)S(1)}, bf16[128,512]{1,0:T(8,128)(2,1)S(1)}, bf16[128,512]{1,0:T(8,128)(2,1)S(1)}) custom-call(s32[16]{0:T(128)} %join.1, bf16[128,2048]{1,0:T(8,128)(2,1)} %tok.1, bf16[128,2048]{1,0:T(8,128)(2,1)} %cot.1, s32[8,128]{1,0:T(8,128)} %bitcast.2, f32[8,128]{1,0:T(8,128)} %bitcast.3, ...), custom_call_target="tpu_custom_call" | custom-call | tf_op jit(solution)/shard_map/expert_step/pallas_call | solution.py:365
  36.8 1.0 %write_out.1 = (bf16[128,2048]{1,0:T(8,128)(2,1)}, bf16[128,512]{1,0:T(8,128)(2,1)}, bf16[128,512]{1,0:T(8,128)(2,1)}, bf16[128,512]{1,0:T(8,128)(2,1)}) custom-call(bf16[128,2048]{1,0:T(8,128)(2,1)S(1)} %get-tuple-element.8.refs_0_, bf16[128,512]{1,0:T(8,128)(2,1)S(1)} %get-tuple-element.9.refs_1_, bf16[128,512]{1,0:T(8,128)(2,1)S(1)} %get-tuple-element.10.refs_2_, ...), custom_call_target="tpu_custom_call" | custom-call | tf_op jit(solution)/shard_map/write_out/pallas_call | solution.py:399

commit v10 on v9

--- a/solution.py
+++ b/solution.py
@@ -245,13 +245,11 @@
         theirs = unit(n, other, slice(None)) if n else unit(0, other)
         copy(theirs, theirs, out.at[8], r3c.at[n], partner).start()
 
-    def gradient(n, q, e, parts):
-        height = members * cap // parts
-        span = slice(e * height, (e + 1) * height)
-        left = rows_all[q].reshape(4, lines, members * cap, depth)[:, :, span]
-        right = all3[n, :, :, span]
-        count = 4 * lines * height
-        return dot(left.reshape(count, depth), right.reshape(count, width), ((0,), (0,)))
+    def gradient(n, q, span, quarters):
+        count = lines * (span.stop - span.start)
+        left = [rows_all[q, k].reshape(lines, members * cap, depth)[:, span].reshape(count, depth) for k in quarters]
+        right = [all3[n, k, :, span].reshape(count, width) for k in quarters]
+        return dot(jnp.concatenate(left, axis=0), jnp.concatenate(right, axis=0), ((0,), (0,)))
 
     gate, up = summed(0), summed(1)
     sig = 1.0 / (1.0 + jnp.exp(-gate))
@@ -293,19 +291,18 @@
             take_in(2, d)
         finish(0)
         output_rows()
-        take_in(1, far)
-        take_in(2, far)
-        finish(1)
-        finish(2)
+        for n in (1, 2):
+            take_in(n, far)
+            finish(n)
 
     @pl.when(inner)
     def _():
         for d in range(1, last):
             take_in(0, d)
         finish(0)
-        for d in range(1, last):
-            take_in(1, d)
-            take_in(2, d)
+        for n in (1, 2):
+            for d in range(1, last):
+                take_in(n, d)
         output_rows()
         finish(1)
         finish(2)
@@ -314,11 +311,13 @@
     from_across(1)
     arrived(rows_all.at[:, 0:3], rx)
     arrived(all3.at[0, 0:2], r3c.at[0])
-    grad_down[...] = gradient(0, 1, 0, 1).astype(BF16)
+    grad_down[...] = gradient(0, 1, slice(0, members * cap), range(4)).astype(BF16)
     arrived(all3.at[0, 0:2], r3c.at[1])
     for n in range(2):
-        half_sum[n] = gradient(1 + n, 0, 0, 2)
+        half_sum[n] = gradient(1 + n, 0, band(2, 0), range(4))
     from_across(2)
+    for n in range(2):
+        half_sum[n] += gradient(1 + n, 0, band(2, 1), (core, 2 + core))
     arrived(send4.at[1:], r4)
     for z in range(lines):
         out_rows = recv4[0, z].astype(F32)
@@ -328,7 +327,7 @@
         mixed[:, z * line_depth : (z + 1) * line_depth] = placed.astype(BF16)
     arrived(all3.at[0, 0:2], r3c.at[2])
     for n, result in enumerate((grad_gate, grad_up)):
-        result[...] = (half_sum[n] + gradient(1 + n, 0, 1, 2)).astype(BF16)
+        result[...] = (half_sum[n] + gradient(1 + n, 0, band(2, 1), (1 - core, 3 - core))).astype(BF16)
 
     for n in range(3):
         departed(wfull.at[:, 0], n)

time: 37.9 us -> 37 us (0.976)
  Pallas kernels: 37.1 us -> 36.2 us
    pallas_call x1, Pallas kernels: 36.1 us -> 35.3 us  [per_device(): pl.pallas_call(functools.partial(kernel, lines, members, cap), out_shape=...]
where the time goes in v10:
time: 37 us; the launch traced here: 36.9 us
  Pallas kernels  36.2 us (98%)
  between operations  0.64 us (2%)
    pallas_call x1, Pallas kernels, per_device(): pl.pallas_call(functools.partial(kernel, lines, members, cap), out_shape=...  35.3 us
    pallas_call x1, Pallas kernels, per_device(): pl.pallas_call(write_out, out_shape=tuple((jax.ShapeDtypeStruct(r.shape,...  0.95 us

profile of v10, /device:TPU:0, one launch (start us, length us, event | category | flops | bytes accessed | tf_op | source)
XLA Modules:
  0.0 36.9 jit_solution(1085078570107216486)
XLA Ops:
  0.6 35.3 %expert_step.1 = (bf16[128,2048]{1,0:T(8,128)(2,1)S(1)}, bf16[128,512]{1,0:T(8,128)(2,1)S(1)}, bf16[128,512]{1,0:T(8,128)(2,1)S(1)}, bf16[128,512]{1,0:T(8,128)(2,1)S(1)}) custom-call(s32[16]{0:T(128)} %join.1, bf16[128,2048]{1,0:T(8,128)(2,1)} %tok.1, bf16[128,2048]{1,0:T(8,128)(2,1)} %cot.1, s32[8,128]{1,0:T(8,128)} %bitcast.2, f32[8,128]{1,0:T(8,128)} %bitcast.3, ...), custom_call_target="tpu_custom_call" | custom-call | tf_op jit(solution)/shard_map/expert_step/pallas_call | solution.py:364
  35.9 1.0 %write_out.1 = (bf16[128,2048]{1,0:T(8,128)(2,1)}, bf16[128,512]{1,0:T(8,128)(2,1)}, bf16[128,512]{1,0:T(8,128)(2,1)}, bf16[128,512]{1,0:T(8,128)(2,1)}) custom-call(bf16[128,2048]{1,0:T(8,128)(2,1)S(1)} %get-tuple-element.8.refs_0_, bf16[128,512]{1,0:T(8,128)(2,1)S(1)} %get-tuple-element.9.refs_1_, bf16[128,512]{1,0:T(8,128)(2,1)S(1)} %get-tuple-element.10.refs_2_, ...), custom_call_target="tpu_custom_call" | custom-call | tf_op jit(solution)/shard_map/write_out/pallas_call | solution.py:398

commit v11 on v10

--- a/solution.py
+++ b/solution.py
@@ -9,7 +9,7 @@
 
 F32, BF16 = jnp.float32, jnp.bfloat16
 MESH = pl.DeviceIdType.MESH
-SPLIT = (1, 1, 2)
+SPLIT, FIRST = (1, 2, 2), (0, 1, 3)
 
 
 def dot(a, b, dims):
@@ -34,11 +34,19 @@
         lax.fori_loop(low, high, lambda i, carry: (body(i), carry)[1], 0)
 
 
+def product_of_rows(rows_all, all3, n, q, span, quarters):
+    lines, height, width = all3.shape[2:]
+    count, depth = lines * (span.stop - span.start), rows_all.shape[-1]
+    left = [rows_all[q, k].reshape(lines, height, depth)[:, span].reshape(count, depth) for k in quarters]
+    right = [all3[n, k, :, span].reshape(count, width) for k in quarters]
+    return dot(jnp.concatenate(left, axis=0), jnp.concatenate(right, axis=0), ((0,), (0,)))
+
+
 def kernel(
     lines, members, cap,
     join, tok, cot, ids, wts, wg, wu, wd,
-    mixed, grad_gate, grad_up, grad_down,
-    joinv, idv, wtv, tokv, cotv, wfull, blk, recv1, rows_all, part, send2, recv2, all3, half_sum, send4, recv4,
+    mixed, grad_down, half_sum, all3, rows_all,
+    joinv, idv, wtv, tokv, cotv, wfull, blk, recv1, part, send2, recv2, send4, recv4,
     local, out, rwy, rwp, r1, rx, r2, r3z, r3y, r3c, r4,
 ):
     p, j = lax.axis_index("dp"), lax.axis_index("expert")
@@ -170,7 +178,7 @@
             span = band(n, e)
             for d in range(1, lines):
                 z, there = on_line(d)
-                recv = r2.at[n + e]
+                recv = r2.at[FIRST[n] + e]
                 copy(send2.at[n, z, span], recv2.at[n, line, span], out.at[4], recv, there).start()
 
     def band(n, e):
@@ -179,7 +187,7 @@
 
     def summed(n, e=0):
         span = band(n, e)
-        arrived(send2.at[n, 1:, span], r2.at[n + e])
+        arrived(send2.at[n, 1:, span], r2.at[FIRST[n] + e])
         total_rows = part[n, line, span]
         for d in range(1, lines):
             total_rows += recv2[n, on_line(d)[0], span].astype(F32)
@@ -207,7 +215,7 @@
         rows_all[q, quarter] = recv1[q, :, quarter]
 
     def unit(n, *place):
-        return all3.at[(0, *place)] if n == 0 else all3.at[(slice(1, 3), *place, band(2, n - 1))]
+        return all3.at[(0 if n < 2 else slice(1, 3), *place, band(2, n % 2))]
 
     def held(n, z):
         return unit(n, quarter, z)
@@ -236,31 +244,29 @@
         copy(held(n, z), held(n, z), out.at[7], r3y.at[n], across).start()
 
     def to_partner(n):
-        mine = unit(n, quarter, slice(None)) if n else unit(0, quarter)
+        mine = unit(n, quarter, slice(None))
         copy(mine, mine, out.at[8], r3c.at[n], partner).start()
 
     def from_across(n):
-        arrived(all3.at[n, 0], r3y.at[n])
+        arrived(unit(n, 0, slice(None)), r3y.at[n])
         other = 2 * (1 - side) + core
-        theirs = unit(n, other, slice(None)) if n else unit(0, other)
+        theirs = unit(n, other, slice(None))
         copy(theirs, theirs, out.at[8], r3c.at[n], partner).start()
 
-    def gradient(n, q, span, quarters):
-        count = lines * (span.stop - span.start)
-        left = [rows_all[q, k].reshape(lines, members * cap, depth)[:, span].reshape(count, depth) for k in quarters]
-        right = [all3[n, k, :, span].reshape(count, width) for k in quarters]
-        return dot(jnp.concatenate(left, axis=0), jnp.concatenate(right, axis=0), ((0,), (0,)))
-
-    gate, up = summed(0), summed(1)
+    gate = summed(0)
     sig = 1.0 / (1.0 + jnp.exp(-gate))
-    all3[0, quarter, line] = (gate * sig * up).astype(BF16)
-    spread_out(0)
-    to_gate, to_up = up * sig * (1.0 + gate * (1.0 - sig)), gate * sig
+    to_hidden, slope = gate * sig, sig * (1.0 + gate * (1.0 - sig))
+    to_gate = []
+    for e in range(2):
+        up, span = summed(1, e), band(2, e)
+        all3[0, quarter, line, span] = (to_hidden[span] * up).astype(BF16)
+        spread_out(e)
+        to_gate.append(up * slope[span])
     for e in range(2):
         dhidden, span = summed(2, e), band(2, e)
-        all3[1, quarter, line, span] = (dhidden * to_gate[span]).astype(BF16)
-        all3[2, quarter, line, span] = (dhidden * to_up[span]).astype(BF16)
-        spread_out(1 + e)
+        all3[1, quarter, line, span] = (dhidden * to_gate[e]).astype(BF16)
+        all3[2, quarter, line, span] = (dhidden * to_hidden[span]).astype(BF16)
+        spread_out(2 + e)
 
     def finish(n):
         take_in(n, last)
@@ -284,40 +290,45 @@
 
     @pl.when(at_end)
     def _():
-        for d in range(1, far + 1):
-            take_in(0, d)
-        for d in range(1, far):
-            take_in(1, d)
-            take_in(2, d)
+        for n in (0, 1):
+            for d in range(1, last):
+                take_in(n, d)
+        for n in (2, 3):
+            for d in range(1, far):
+                take_in(n, d)
         finish(0)
+        finish(1)
         output_rows()
-        for n in (1, 2):
+        for n in (2, 3):
             take_in(n, far)
             finish(n)
 
     @pl.when(inner)
     def _():
-        for d in range(1, last):
-            take_in(0, d)
+        for n in (0, 1):
+            for d in range(1, last):
+                take_in(n, d)
         finish(0)
-        for n in (1, 2):
+        finish(1)
+        for n in (2, 3):
             for d in range(1, last):
                 take_in(n, d)
         output_rows()
-        finish(1)
         finish(2)
-
-    from_across(0)
-    from_across(1)
+        finish(3)
+
+    for n in range(3):
+        from_across(n)
     arrived(rows_all.at[:, 0:3], rx)
-    arrived(all3.at[0, 0:2], r3c.at[0])
-    grad_down[...] = gradient(0, 1, slice(0, members * cap), range(4)).astype(BF16)
-    arrived(all3.at[0, 0:2], r3c.at[1])
     for n in range(2):
-        half_sum[n] = gradient(1 + n, 0, band(2, 0), range(4))
-    from_across(2)
+        arrived(unit(n, slice(0, 2), slice(None)), r3c.at[n])
+    grad_down[...] = product_of_rows(rows_all, all3, 0, 1, slice(0, members * cap), range(4)).astype(BF16)
+    arrived(unit(2, slice(0, 2), slice(None)), r3c.at[2])
     for n in range(2):
-        half_sum[n] += gradient(1 + n, 0, band(2, 1), (core, 2 + core))
+        half_sum[n] = product_of_rows(rows_all, all3, 1 + n, 0, band(2, 0), range(4))
+    from_across(3)
+    for n in range(2):
+        half_sum[n] += product_of_rows(rows_all, all3, 1 + n, 0, band(2, 1), (core, 2 + core))
     arrived(send4.at[1:], r4)
     for z in range(lines):
         out_rows = recv4[0, z].astype(F32)
@@ -325,9 +336,7 @@
             out_rows += recv4[m, z].astype(F32)
         placed = dot(spread, (out_rows * slot_weight).astype(BF16), ((1,), (0,)))
         mixed[:, z * line_depth : (z + 1) * line_depth] = placed.astype(BF16)
-    arrived(all3.at[0, 0:2], r3c.at[2])
-    for n, result in enumerate((grad_gate, grad_up)):
-        result[...] = (half_sum[n] + gradient(1 + n, 0, band(2, 1), (1 - core, 3 - core))).astype(BF16)
+    arrived(unit(3, slice(0, 2), slice(None)), r3c.at[3])
 
     for n in range(3):
         departed(wfull.at[:, 0], n)
@@ -342,11 +351,21 @@
     departed(send4.at[1:], 9)
 
 
-def write_out(*refs):
-    sems = refs[-1]
-    copies = [pltpu.make_async_copy(refs[n], refs[4 + n], sems.at[n]) for n in range(4)]
-    for c in copies:
-        c.start()
+def write_out(mixed, grad_down, half_sum, all3, rows_all, mixed_out, gate_out, up_out, down_out, last_two, sems):
+    core = lax.rem(lax.axis_index("dp"), 2)
+    height = all3.shape[3]
+    copies = [
+        pltpu.make_async_copy(src, dst, sems.at[n])
+        for n, (src, dst) in enumerate(
+            ((mixed, mixed_out), (grad_down, down_out), (last_two.at[0], gate_out), (last_two.at[1], up_out))
+        )
+    ]
+    copies[0].start()
+    copies[1].start()
+    for n in range(2):
+        rest = product_of_rows(rows_all, all3, 1 + n, 0, slice(height // 2, height), (1 - core, 3 - core))
+        last_two[n] = (half_sum[n] + rest).astype(BF16)
+        copies[2 + n].start()
     for c in copies:
         c.wait()
 
@@ -358,14 +377,20 @@
     total = lines * members
     rows = members * cap
     vmem = pl.BlockSpec(memory_space=pltpu.VMEM)
-    hbm = pl.BlockSpec(memory_space=pl.ANY)
+    hbm = pl.BlockSpec(memory_space=pltpu.HBM)
     dma = pltpu.SemaphoreType.DMA
-    grad = pltpu.VMEM((depth, width), BF16)
+    grad = jax.ShapeDtypeStruct((depth, width), BF16)
     results = pl.pallas_call(
         functools.partial(kernel, lines, members, cap),
-        out_shape=(pltpu.VMEM((tok_count, model), BF16), grad, grad, grad),
+        out_shape=(
+            pltpu.VMEM((tok_count, model), BF16),
+            pltpu.VMEM((depth, width), BF16),
+            pltpu.VMEM((2, depth, width), F32),
+            pltpu.VMEM((3, 4, lines, rows, width), BF16),
+            pltpu.VMEM((2, 4, total, cap, depth), BF16),
+        ),
         in_specs=[hbm] * 8,
-        out_specs=(vmem,) * 4,
+        out_specs=(vmem,) * 5,
         scratch_shapes=[
             pltpu.SMEM(join_groups.shape, jnp.int32),
             pltpu.VMEM(expert_ids.shape[::-1], jnp.int32),
@@ -375,32 +400,35 @@
             pltpu.VMEM((3, 4, depth, width), BF16),
             pltpu.VMEM((2, lines, 4, cap, depth), BF16),
             pltpu.VMEM((2, total, 4, cap, depth), BF16),
-            pltpu.VMEM((2, 4, total, cap, depth), BF16),
             pltpu.VMEM((3, lines, rows, width), F32),
             pltpu.VMEM((3, lines, rows, width), BF16),
             pltpu.VMEM((3, lines, rows, width), BF16),
-            pltpu.VMEM((3, 4, lines, rows, width), BF16),
-            pltpu.VMEM((2, depth, width), F32),
             pltpu.VMEM((total, cap, 4 * depth), BF16),
             pltpu.VMEM((members, lines, cap, 4 * depth), BF16),
             dma((6,)), dma((12,)),
             dma((3,)), dma((3,)),
             dma((2,)), dma(()),
-            dma((4,)),
-            dma((3, lines - 1)), dma((3,)), dma((3,)),
+            dma((5,)),
+            dma((4, lines - 1)), dma((4,)), dma((4,)),
             dma(()),
         ],
         compiler_params=pltpu.CompilerParams(
-            collective_id=0, has_side_effects=True, vmem_limit_bytes=60 * 1024 * 1024
+            collective_id=0, has_side_effects=True, vmem_limit_bytes=44 * 1024 * 1024
         ),
         name="expert_step",
-    )(join_groups, tokens, cotangent, expert_ids.T, route_weights.T, w_gate, w_up, w_down)
+    )(
+        *(
+            pltpu.with_memory_space_constraint(x, pltpu.HBM)
+            for x in (join_groups, tokens, cotangent, expert_ids.T, route_weights.T, w_gate, w_up, w_down)
+        )
+    )
     return pl.pallas_call(
         write_out,
-        out_shape=tuple(jax.ShapeDtypeStruct(r.shape, r.dtype) for r in results),
-        in_specs=[vmem] * 4,
+        out_shape=(jax.ShapeDtypeStruct((tok_count, model), BF16), grad, grad, grad),
+        in_specs=[vmem] * 5,
         out_specs=(hbm,) * 4,
-        scratch_shapes=[dma((4,))],
+        scratch_shapes=[pltpu.VMEM((2, depth, width), BF16), dma((4,))],
+        compiler_params=pltpu.CompilerParams(vmem_limit_bytes=16 * 1024 * 1024),
         name="write_out",
     )(*(pltpu.with_memory_space_constraint(r, pltpu.VMEM) for r in results))
 

time: 37 us -> 36.7 us (level)
    pallas_call x1, Pallas kernels: 35.3 us -> 34.9 us  [per_device(): pl.pallas_call(functools.partial(kernel, lines, members, cap), out_shape=...]
where the time goes in v11:
time: 36.7 us; the launch traced here: 36.5 us
  Pallas kernels  35.9 us (98%)
  between operations  0.64 us (2%)
    pallas_call x1, Pallas kernels, per_device(): pl.pallas_call(functools.partial(kernel, lines, members, cap), out_shape=...  34.9 us
    pallas_call x1, Pallas kernels, per_device(): pl.pallas_call(write_out, out_shape=(jax.ShapeDtypeStruct((tok_count, mod...  0.97 us

profile of v11, /device:TPU:0, one launch (start us, length us, event | category | flops | bytes accessed | tf_op | source)
XLA Modules:
  0.0 36.5 jit_solution(6609578145625928148)
XLA Ops:
  0.6 34.9 %expert_step.1 = (bf16[128,2048]{1,0:T(8,128)(2,1)S(1)}, bf16[128,512]{1,0:T(8,128)(2,1)S(1)}, f32[2,128,512]{2,1,0:T(8,128)S(1)}, bf16[3,4,4,32,512]{4,3,2,1,0:...) custom-call(s32[16]{0:T(128)} %join.1, bf16[128,2048]{1,0:T(8,128)(2,1)} %tok.1, bf16[128,2048]{1,0:T(8,128)(2,1)} %cot.1, ...), custom_call_target="tpu_custom_call" | custom-call | tf_op jit(solution)/shard_map/expert_step/pallas_call | solution.py:383
  35.5 1.0 %write_out.1 = (bf16[128,2048]{1,0:T(8,128)(2,1)}, bf16[128,512]{1,0:T(8,128)(2,1)}, bf16[128,512]{1,0:T(8,128)(2,1)}, bf16[128,512]{1,0:T(8,128)(2,1)}) custom-call(bf16[128,2048]{1,0:T(8,128)(2,1)S(1)} %get-tuple-element.9.mixed, bf16[128,512]{1,0:T(8,128)(2,1)S(1)} %get-tuple-element.10.grad_down, f32[2,128,512]{2,1,0:T(8,128)S(1)} %get-tuple-element.11.half_sum, ...), custom_call_target="tpu_custom_call" | custom-call | tf_op jit(solution)/shard_map/write_out/pallas_call | solution.py:425

commit v12 on v11

--- a/solution.py
+++ b/solution.py
@@ -317,18 +317,17 @@
         finish(2)
         finish(3)
 
-    for n in range(3):
+    for n in range(4):
         from_across(n)
     arrived(rows_all.at[:, 0:3], rx)
+    for n in range(2):
+        half_sum[n] = product_of_rows(rows_all, all3, 1 + n, 0, band(2, 1), (core, 2 + core))
     for n in range(2):
         arrived(unit(n, slice(0, 2), slice(None)), r3c.at[n])
     grad_down[...] = product_of_rows(rows_all, all3, 0, 1, slice(0, members * cap), range(4)).astype(BF16)
     arrived(unit(2, slice(0, 2), slice(None)), r3c.at[2])
     for n in range(2):
-        half_sum[n] = product_of_rows(rows_all, all3, 1 + n, 0, band(2, 0), range(4))
-    from_across(3)
-    for n in range(2):
-        half_sum[n] += product_of_rows(rows_all, all3, 1 + n, 0, band(2, 1), (core, 2 + core))
+        half_sum[n] += product_of_rows(rows_all, all3, 1 + n, 0, band(2, 0), range(4))
     arrived(send4.at[1:], r4)
     for z in range(lines):
         out_rows = recv4[0, z].astype(F32)

time: 36.7 us -> 36.4 us (level)
  no operation moved by 1% of the time
where the time goes in v12:
time: 36.4 us; the launch traced here: 36.2 us
  Pallas kernels  35.6 us (98%)
  between operations  0.64 us (2%)
    pallas_call x1, Pallas kernels, per_device(): pl.pallas_call(functools.partial(kernel, lines, members, cap), out_shape=...  34.6 us
    pallas_call x1, Pallas kernels, per_device(): pl.pallas_call(write_out, out_shape=(jax.ShapeDtypeStruct((tok_count, mod...  0.97 us

profile of v12, /device:TPU:0, one launch (start us, length us, event | category | flops | bytes accessed | tf_op | source)
XLA Modules:
  0.0 36.2 jit_solution(6085144521052426433)
XLA Ops:
  0.6 34.6 %expert_step.1 = (bf16[128,2048]{1,0:T(8,128)(2,1)S(1)}, bf16[128,512]{1,0:T(8,128)(2,1)S(1)}, f32[2,128,512]{2,1,0:T(8,128)S(1)}, bf16[3,4,4,32,512]{4,3,2,1,0:...) custom-call(s32[16]{0:T(128)} %join.1, bf16[128,2048]{1,0:T(8,128)(2,1)} %tok.1, bf16[128,2048]{1,0:T(8,128)(2,1)} %cot.1, ...), custom_call_target="tpu_custom_call" | custom-call | tf_op jit(solution)/shard_map/expert_step/pallas_call | solution.py:382
  35.2 1.0 %write_out.1 = (bf16[128,2048]{1,0:T(8,128)(2,1)}, bf16[128,512]{1,0:T(8,128)(2,1)}, bf16[128,512]{1,0:T(8,128)(2,1)}, bf16[128,512]{1,0:T(8,128)(2,1)}) custom-call(bf16[128,2048]{1,0:T(8,128)(2,1)S(1)} %get-tuple-element.9.mixed, bf16[128,512]{1,0:T(8,128)(2,1)S(1)} %get-tuple-element.10.grad_down, f32[2,128,512]{2,1,0:T(8,128)S(1)} %get-tuple-element.11.half_sum, ...), custom_call_target="tpu_custom_call" | custom-call | tf_op jit(solution)/shard_map/write_out/pallas_call | solution.py:424

commit v13 on v12

--- a/solution.py
+++ b/solution.py
@@ -94,7 +94,8 @@
         pl.semaphore_signal(barrier, inc=1, device_id=device(z, side, core, member), device_id_type=MESH)
 
     each(1, total, greet)
-    for there in [beside(n)[1] for n in range(3)]:
+    slanted = device(flip(line, 1, lines), 1 - side, core, j)
+    for there in [beside(n)[1] for n in range(3)] + [slanted]:
         pl.semaphore_signal(barrier, inc=1, device_id=there, device_id_type=MESH)
 
     loads = [
@@ -151,7 +152,7 @@
     def departed(ref, n):
         copy(ref, ref, out.at[n], rx, partner).wait_send()
 
-    pl.semaphore_wait(barrier, total - 1 + 3)
+    pl.semaphore_wait(barrier, total - 1 + 4)
 
     swap(0).start()
     loads[3].wait()
@@ -234,14 +235,19 @@
                 block(n, line, d, out.at[6], on_line(d)[1]).start()
         for n in which:
             pl.when(inner)(block(n, line, last, out.at[10], on_line(last)[1]).start)
-            copy(held(n, line), held(n, line), out.at[7], r3y.at[n], across).start()
+            copy(held(n, line), held(n, line), out.at[14 if n == 3 else 7], r3y.at[n], across).start()
 
     def take_in(n, d):
         z, there = on_line(d)
         block(n, z, d, out.at[6], there).wait_recv()
         if d == last - 1:
             pl.when(beside_end)(block(n, z, last, out.at[11], on_line(1)[1]).start)
-        copy(held(n, z), held(n, z), out.at[7], r3y.at[n], across).start()
+        if n == 3 and d == last - 1:
+            pl.when(beside_end)(copy(held(n, z), held(n, z), out.at[13], r3y.at[n], slanted).start)
+        if n == 3 and d == last:
+            pl.when(inner)(copy(held(n, z), held(n, z), out.at[12], r3y.at[n], across).start)
+        else:
+            copy(held(n, z), held(n, z), out.at[14 if n == 3 else 7], r3y.at[n], across).start()
 
     def to_partner(n):
         mine = unit(n, quarter, slice(None))
@@ -345,7 +351,10 @@
     departed(all3.at[:, 0, 1:last], 6)
     pl.when(inner)(functools.partial(departed, all3.at[:, 0, 0], 10))
     pl.when(beside_end)(functools.partial(departed, all3.at[:, 0, 0], 11))
-    departed(all3.at[:, 0], 7)
+    departed(all3.at[0:2, 0], 7)
+    departed(all3.at[0, 0, 1:], 14)
+    pl.when(inner)(functools.partial(departed, all3.at[0, 0, 0], 12))
+    pl.when(beside_end)(functools.partial(departed, all3.at[0, 0, 0], 13))
     departed(all3.at[:, 0:2], 8)
     departed(send4.at[1:], 9)
 
@@ -404,7 +413,7 @@
             pltpu.VMEM((3, lines, rows, width), BF16),
             pltpu.VMEM((total, cap, 4 * depth), BF16),
             pltpu.VMEM((members, lines, cap, 4 * depth), BF16),
-            dma((6,)), dma((12,)),
+            dma((6,)), dma((15,)),
             dma((3,)), dma((3,)),
             dma((2,)), dma(()),
             dma((5,)),

time: 36.4 us -> 36.2 us (level)
  no operation moved by 1% of the time
where the time goes in v13:
time: 36.2 us; the launch traced here: 35.9 us
  Pallas kernels  35.3 us (98%)
  between operations  0.64 us (2%)
    pallas_call x1, Pallas kernels, per_device(): pl.pallas_call(functools.partial(kernel, lines, members, cap), out_shape=...  34.3 us
    pallas_call x1, Pallas kernels, per_device(): pl.pallas_call(write_out, out_shape=(jax.ShapeDtypeStruct((tok_count, mod...  0.97 us

profile of v13, /device:TPU:0, one launch (start us, length us, event | category | flops | bytes accessed | tf_op | source)
XLA Modules:
  0.0 35.9 jit_solution(7955707996634847624)
XLA Ops:
  0.6 34.3 %expert_step.1 = (bf16[128,2048]{1,0:T(8,128)(2,1)S(1)}, bf16[128,512]{1,0:T(8,128)(2,1)S(1)}, f32[2,128,512]{2,1,0:T(8,128)S(1)}, bf16[3,4,4,32,512]{4,3,2,1,0:...) custom-call(s32[16]{0:T(128)} %join.1, bf16[128,2048]{1,0:T(8,128)(2,1)} %tok.1, bf16[128,2048]{1,0:T(8,128)(2,1)} %cot.1, ...), custom_call_target="tpu_custom_call" | custom-call | tf_op jit(solution)/shard_map/expert_step/pallas_call | solution.py:391
  35.0 1.0 %write_out.1 = (bf16[128,2048]{1,0:T(8,128)(2,1)}, bf16[128,512]{1,0:T(8,128)(2,1)}, bf16[128,512]{1,0:T(8,128)(2,1)}, bf16[128,512]{1,0:T(8,128)(2,1)}) custom-call(bf16[128,2048]{1,0:T(8,128)(2,1)S(1)} %get-tuple-element.9.mixed, bf16[128,512]{1,0:T(8,128)(2,1)S(1)} %get-tuple-element.10.grad_down, f32[2,128,512]{2,1,0:T(8,128)S(1)} %get-tuple-element.11.half_sum, ...), custom_call_target="tpu_custom_call" | custom-call | tf_op jit(solution)/shard_map/write_out/pallas_call | solution.py:433

commit v14 on v13

--- a/solution.py
+++ b/solution.py
@@ -235,19 +235,19 @@
                 block(n, line, d, out.at[6], on_line(d)[1]).start()
         for n in which:
             pl.when(inner)(block(n, line, last, out.at[10], on_line(last)[1]).start)
-            copy(held(n, line), held(n, line), out.at[14 if n == 3 else 7], r3y.at[n], across).start()
+            copy(held(n, line), held(n, line), out.at[14 if n >= 2 else 7], r3y.at[n], across).start()
 
     def take_in(n, d):
         z, there = on_line(d)
         block(n, z, d, out.at[6], there).wait_recv()
         if d == last - 1:
             pl.when(beside_end)(block(n, z, last, out.at[11], on_line(1)[1]).start)
-        if n == 3 and d == last - 1:
+        if n >= 2 and d == last - 1:
             pl.when(beside_end)(copy(held(n, z), held(n, z), out.at[13], r3y.at[n], slanted).start)
-        if n == 3 and d == last:
+        if n >= 2 and d == last:
             pl.when(inner)(copy(held(n, z), held(n, z), out.at[12], r3y.at[n], across).start)
         else:
-            copy(held(n, z), held(n, z), out.at[14 if n == 3 else 7], r3y.at[n], across).start()
+            copy(held(n, z), held(n, z), out.at[14 if n >= 2 else 7], r3y.at[n], across).start()
 
     def to_partner(n):
         mine = unit(n, quarter, slice(None))
@@ -351,10 +351,10 @@
     departed(all3.at[:, 0, 1:last], 6)
     pl.when(inner)(functools.partial(departed, all3.at[:, 0, 0], 10))
     pl.when(beside_end)(functools.partial(departed, all3.at[:, 0, 0], 11))
-    departed(all3.at[0:2, 0], 7)
-    departed(all3.at[0, 0, 1:], 14)
-    pl.when(inner)(functools.partial(departed, all3.at[0, 0, 0], 12))
-    pl.when(beside_end)(functools.partial(departed, all3.at[0, 0, 0], 13))
+    departed(all3.at[0, 0], 7)
+    departed(all3.at[0:2, 0, 1:], 14)
+    pl.when(inner)(functools.partial(departed, all3.at[0:2, 0, 0], 12))
+    pl.when(beside_end)(functools.partial(departed, all3.at[0:2, 0, 0], 13))
     departed(all3.at[:, 0:2], 8)
     departed(send4.at[1:], 9)
 

time: 36.2 us -> 36 us (level)
  no operation moved by 1% of the time
where the time goes in v14:
time: 36 us; the launch traced here: 35.9 us
  Pallas kernels  35.2 us (98%)
  between operations  0.64 us (2%)
    pallas_call x1, Pallas kernels, per_device(): pl.pallas_call(functools.partial(kernel, lines, members, cap), out_shape=...  34.2 us
    pallas_call x1, Pallas kernels, per_device(): pl.pallas_call(write_out, out_shape=(jax.ShapeDtypeStruct((tok_count, mod...  0.97 us

profile of v14, /device:TPU:0, one launch (start us, length us, event | category | flops | bytes accessed | tf_op | source)
XLA Modules:
  0.0 35.9 jit_solution(9306541833076133034)
XLA Ops:
  0.6 34.2 %expert_step.1 = (bf16[128,2048]{1,0:T(8,128)(2,1)S(1)}, bf16[128,512]{1,0:T(8,128)(2,1)S(1)}, f32[2,128,512]{2,1,0:T(8,128)S(1)}, bf16[3,4,4,32,512]{4,3,2,1,0:...) custom-call(s32[16]{0:T(128)} %join.1, bf16[128,2048]{1,0:T(8,128)(2,1)} %tok.1, bf16[128,2048]{1,0:T(8,128)(2,1)} %cot.1, ...), custom_call_target="tpu_custom_call" | custom-call | tf_op jit(solution)/shard_map/expert_step/pallas_call | solution.py:391
  34.9 1.0 %write_out.1 = (bf16[128,2048]{1,0:T(8,128)(2,1)}, bf16[128,512]{1,0:T(8,128)(2,1)}, bf16[128,512]{1,0:T(8,128)(2,1)}, bf16[128,512]{1,0:T(8,128)(2,1)}) custom-call(bf16[128,2048]{1,0:T(8,128)(2,1)S(1)} %get-tuple-element.9.mixed, bf16[128,512]{1,0:T(8,128)(2,1)S(1)} %get-tuple-element.10.grad_down, f32[2,128,512]{2,1,0:T(8,128)S(1)} %get-tuple-element.11.half_sum, ...), custom_call_target="tpu_custom_call" | custom-call | tf_op jit(solution)/shard_map/write_out/pallas_call | solution.py:433

commit v15 on v14

--- a/solution.py
+++ b/solution.py
@@ -93,7 +93,7 @@
         z, member = peer(t)
         pl.semaphore_signal(barrier, inc=1, device_id=device(z, side, core, member), device_id_type=MESH)
 
-    each(1, total, greet)
+    each(1, total, lambda t: greet(total - t))
     slanted = device(flip(line, 1, lines), 1 - side, core, j)
     for there in [beside(n)[1] for n in range(3)] + [slanted]:
         pl.semaphore_signal(barrier, inc=1, device_id=there, device_id_type=MESH)
@@ -130,11 +130,11 @@
         return copy(wfull.at[n, quarter], wfull.at[n, quarter], out.at[0], rwy.at[n], across)
 
     def lend(n):
-        return copy(wfull.at[n, quarter], wfull.at[n, quarter], out.at[1], rwp.at[n], partner)
+        return copy(wfull.at[n, quarter], wfull.at[n, quarter], out.at[0], rwp.at[n], partner)
 
     def relay(n):
         held = wfull.at[n, 2 * (1 - side) + core]
-        return copy(held, held, out.at[2], rwp.at[n], partner)
+        return copy(held, held, out.at[0], rwp.at[n], partner)
 
     def give(q, t):
         z, member = peer(t)
@@ -235,7 +235,7 @@
                 block(n, line, d, out.at[6], on_line(d)[1]).start()
         for n in which:
             pl.when(inner)(block(n, line, last, out.at[10], on_line(last)[1]).start)
-            copy(held(n, line), held(n, line), out.at[14 if n >= 2 else 7], r3y.at[n], across).start()
+            copy(held(n, line), held(n, line), out.at[2 if n >= 2 else 7], r3y.at[n], across).start()
 
     def take_in(n, d):
         z, there = on_line(d)
@@ -243,11 +243,11 @@
         if d == last - 1:
             pl.when(beside_end)(block(n, z, last, out.at[11], on_line(1)[1]).start)
         if n >= 2 and d == last - 1:
-            pl.when(beside_end)(copy(held(n, z), held(n, z), out.at[13], r3y.at[n], slanted).start)
+            pl.when(beside_end)(copy(held(n, z), held(n, z), out.at[1], r3y.at[n], slanted).start)
         if n >= 2 and d == last:
             pl.when(inner)(copy(held(n, z), held(n, z), out.at[12], r3y.at[n], across).start)
         else:
-            copy(held(n, z), held(n, z), out.at[14 if n >= 2 else 7], r3y.at[n], across).start()
+            copy(held(n, z), held(n, z), out.at[2 if n >= 2 else 7], r3y.at[n], across).start()
 
     def to_partner(n):
         mine = unit(n, quarter, slice(None))
@@ -343,8 +343,7 @@
         mixed[:, z * line_depth : (z + 1) * line_depth] = placed.astype(BF16)
     arrived(unit(3, slice(0, 2), slice(None)), r3c.at[3])
 
-    for n in range(3):
-        departed(wfull.at[:, 0], n)
+    departed(wfull.at[:, 0:3], 0)
     departed(recv1.at[:, 1:], 3)
     departed(send2.at[:, 1:], 4)
     departed(rows_all.at[:, 0:3], 5)
@@ -352,9 +351,9 @@
     pl.when(inner)(functools.partial(departed, all3.at[:, 0, 0], 10))
     pl.when(beside_end)(functools.partial(departed, all3.at[:, 0, 0], 11))
     departed(all3.at[0, 0], 7)
-    departed(all3.at[0:2, 0, 1:], 14)
+    departed(all3.at[0:2, 0, 1:], 2)
     pl.when(inner)(functools.partial(departed, all3.at[0:2, 0, 0], 12))
-    pl.when(beside_end)(functools.partial(departed, all3.at[0:2, 0, 0], 13))
+    pl.when(beside_end)(functools.partial(departed, all3.at[0:2, 0, 0], 1))
     departed(all3.at[:, 0:2], 8)
     departed(send4.at[1:], 9)
 
@@ -413,7 +412,7 @@
             pltpu.VMEM((3, lines, rows, width), BF16),
             pltpu.VMEM((total, cap, 4 * depth), BF16),
             pltpu.VMEM((members, lines, cap, 4 * depth), BF16),
-            dma((6,)), dma((15,)),
+            dma((6,)), dma((13,)),
             dma((3,)), dma((3,)),
             dma((2,)), dma(()),
             dma((5,)),

time: 36 us -> 36.1 us (level)
  no operation moved by 1% of the time
where the time goes in v15:
time: 36.1 us; the launch traced here: 35.9 us
  Pallas kernels  35.2 us (98%)
  between operations  0.64 us (2%)
    pallas_call x1, Pallas kernels, per_device(): pl.pallas_call(functools.partial(kernel, lines, members, cap), out_shape=...  34.3 us
    pallas_call x1, Pallas kernels, per_device(): pl.pallas_call(write_out, out_shape=(jax.ShapeDtypeStruct((tok_count, mod...  0.97 us

profile of v15, /device:TPU:0, one launch (start us, length us, event | category | flops | bytes accessed | tf_op | source)
XLA Modules:
  0.0 35.9 jit_solution(2541483976891619670)
XLA Ops:
  0.6 34.3 %expert_step.1 = (bf16[128,2048]{1,0:T(8,128)(2,1)S(1)}, bf16[128,512]{1,0:T(8,128)(2,1)S(1)}, f32[2,128,512]{2,1,0:T(8,128)S(1)}, bf16[3,4,4,32,512]{4,3,2,1,0:...) custom-call(s32[16]{0:T(128)} %join.1, bf16[128,2048]{1,0:T(8,128)(2,1)} %tok.1, bf16[128,2048]{1,0:T(8,128)(2,1)} %cot.1, ...), custom_call_target="tpu_custom_call" | custom-call | tf_op jit(solution)/shard_map/expert_step/pallas_call | solution.py:390
  34.9 1.0 %write_out.1 = (bf16[128,2048]{1,0:T(8,128)(2,1)}, bf16[128,512]{1,0:T(8,128)(2,1)}, bf16[128,512]{1,0:T(8,128)(2,1)}, bf16[128,512]{1,0:T(8,128)(2,1)}) custom-call(bf16[128,2048]{1,0:T(8,128)(2,1)S(1)} %get-tuple-element.9.mixed, bf16[128,512]{1,0:T(8,128)(2,1)S(1)} %get-tuple-element.10.grad_down, f32[2,128,512]{2,1,0:T(8,128)S(1)} %get-tuple-element.11.half_sum, ...), custom_call_target="tpu_custom_call" | custom-call | tf_op jit(solution)/shard_map/write_out/pallas_call | solution.py:432
